TPU v7x, 256 devices: a whole 4x4x8 slice. The times are simulated.
256 devices in a mesh: blk: 32 (over z, y), rep: 8 (over x, core).
Axes of the slice: x: 4, y: 4, z: 8, core: 2. Of those that a mesh axis runs over, the one named last changes fastest.
Arguments:
- features: bfloat16 [16384, 1024], P('blk'), may hold values from -8 to 8
- node_order: int32 [16384], P('blk'), may hold values from 0 to 511, as said below
- adj_tiles: bfloat16 [32, 8, 4, 4, 256, 256], P('blk', 'rep'), may hold values from -0.0703125 to 0.1171875
- counts: int32 [32, 8, 4], P('blk', 'rep'), may hold values from 0 to 4, as said below
- coords: int32 [32, 8, 4, 4, 2], P('blk', 'rep'), may hold values from 0 to 1, as said below
- w_self: bfloat16 [1024, 1024], replicated, may hold values from -0.1875 to 0.1875
- w_neigh: bfloat16 [1024, 1024], replicated, may hold values from -0.1875 to 0.1875
- norm_gain: float32 [1024], P('rep'), may hold values from 0.5 to 1.5
- norm_bias: float32 [1024], P('rep'), may hold values from -0.5 to 0.5
- mean_scale: float32 [1024], P('rep'), may hold values from 0.2 to 1
- cotangent: bfloat16 [16384, 1024], P('blk', 'rep'), may hold values from -10 to 10
Outputs:
- normed: bfloat16 [16384, 1024], P('blk', 'rep')
- grad_feats: bfloat16 [16384, 1024], P(('blk', 'rep'))
- grad_neigh: float32 [1024, 1024], P('blk', 'rep')
- grad_norm: float32 [3, 1024], P(None, 'rep')
Inputs may be any that keep to these rules, and one draw needn't show every extreme that they name: `node_order`: each aligned run of 512 entries holds every number 0 to 511 once. `counts`: in every draw some row block, replica and step has all 4 slots live. `coords`: the 4 pairs of row tile and column tile of one row block, replica and step are distinct.
All inputs are finite; a program needn't handle non-finite values.
Results may differ from a plain program's by a relative error of at most 0.017.
Values may be sent and summed in bfloat16 or wider, within the bound.
A program may use at most 128 MiB of HBM per device.

v0:
```python
import jax
import jax.numpy as jnp
from jax import lax
from jax.sharding import PartitionSpec as P

EPSILON = 1e-05
PRECISE = lax.Precision.HIGHEST


def shifted(x, axis, by):
    size = lax.axis_size(axis)
    return lax.ppermute(x, axis, [(i, (i + by) % size) for i in range(size)])


def body(
    features,
    node_order,
    adj_tiles,
    counts,
    coords,
    w_self,
    w_neigh,
    norm_gain,
    norm_bias,
    mean_scale,
    cotangent,
):
    block_count = lax.axis_size("blk")
    rep_count = lax.axis_size("rep")
    pass_count = block_count // rep_count
    rep_bits = rep_count.bit_length() - 1
    rep_index = lax.axis_index("rep")
    rows_blk, feat_width = features.shape
    col_width = cotangent.shape[1]
    tile_size = adj_tiles.shape[-1]
    slot_count = adj_tiles.shape[3]
    tile_cols = rows_blk // tile_size
    node_count = rows_blk * block_count
    own_tiles = adj_tiles.reshape(pass_count, slot_count, tile_size, tile_size)
    own_counts = counts.reshape(pass_count)
    own_pos = coords.reshape(pass_count, slot_count, 2)
    slot_ids = jnp.arange(slot_count, dtype=jnp.int32)
    tile_ids = jnp.arange(tile_cols, dtype=jnp.int32)
    empty = jnp.zeros((tile_cols, tile_size, feat_width), jnp.float32)
    by_rows = (((1,), (1,)), ((), ()))
    by_nodes = (((0,), (0,)), ((), ()))
    reordered = jnp.take(features, node_order, axis=0)
    moving = reordered
    for shift_bit in range(rep_bits):
        arrived = shifted(moving, "blk", 1 << shift_bit)
        moving = jnp.where(rep_index >> shift_bit & 1 == 1, arrived, moving)
    partial_value = empty
    for pass_idx in range(pass_count):
        gather_blk_tiles = own_tiles[pass_idx]
        gather_slot_pos = own_pos[pass_idx]
        gather_live_count = own_counts[pass_idx]
        source = moving.reshape(tile_cols, tile_size, feat_width)
        gathered = source[gather_slot_pos[:, 1]]
        gather_product = jnp.einsum(
            "tab,tbd->tad", gather_blk_tiles, gathered, preferred_element_type=jnp.float32
        )
        gather_select = (
            (gather_slot_pos[None, :, 0] == tile_ids[:, None])
            & (slot_ids[None, :] < gather_live_count)
        ).astype(jnp.float32)
        partial_value = partial_value + jnp.einsum(
            "qt,tad->qad", gather_select, gather_product, precision=PRECISE
        )
        if pass_idx + 1 < pass_count:
            moving = shifted(moving, "blk", rep_count)
    agg_rows = lax.psum(partial_value.reshape(rows_blk, feat_width), "rep")
    aggregate = agg_rows.astype(jnp.bfloat16)
    col_start = rep_index * col_width
    self_cols = lax.dynamic_slice_in_dim(w_self, col_start, col_width, 1)
    neigh_cols = lax.dynamic_slice_in_dim(w_neigh, col_start, col_width, 1)
    pre_norm = jnp.dot(reordered, self_cols, preferred_element_type=jnp.float32) + jnp.dot(
        aggregate, neigh_cols, preferred_element_type=jnp.float32
    )
    upstream = cotangent.astype(jnp.float32)
    col_mean = lax.psum(jnp.sum(pre_norm, axis=0), "blk") / node_count
    centered = pre_norm - mean_scale * col_mean
    spread = lax.psum(jnp.sum(centered * centered, axis=0), "blk") / node_count
    cot_sum, cot_cent = lax.psum(
        (jnp.sum(upstream, axis=0), jnp.sum(upstream * centered, axis=0)), "blk"
    )
    col_scale = jnp.sqrt(spread + EPSILON)
    normed = (norm_gain * centered / col_scale + norm_bias).astype(jnp.bfloat16)
    grad_centered = norm_gain * upstream / col_scale - centered * (
        norm_gain * cot_cent / (node_count * col_scale**3)
    )
    grad_cent_total = (
        norm_gain * cot_sum / col_scale
        - (1.0 - mean_scale) * col_mean * norm_gain * cot_cent / col_scale**3
    )
    grad_pre = (grad_centered - mean_scale * grad_cent_total / node_count).astype(jnp.bfloat16)
    agg_share = lax.dot_general(grad_pre, neigh_cols, by_rows, preferred_element_type=jnp.float32)
    grad_agg = lax.psum(agg_share.astype(jnp.bfloat16), "rep")
    self_share = lax.dot_general(grad_pre, self_cols, by_rows, preferred_element_type=jnp.float32)
    weight_term = lax.dot_general(aggregate, grad_pre, by_nodes, preferred_element_type=jnp.float32)
    grad_neigh = (
        lax.psum_scatter(
            weight_term.astype(jnp.bfloat16), "blk", scatter_dimension=0, tiled=True
        ).astype(jnp.float32)
        / node_count
    )
    grad_source = grad_agg.reshape(tile_cols, tile_size, feat_width)
    carried = empty
    for pass_idx in reversed(range(pass_count)):
        blk_tiles = own_tiles[pass_idx]
        slot_pos = own_pos[pass_idx]
        live_count = own_counts[pass_idx]
        row_data = grad_source[slot_pos[:, 0]]
        product = jnp.einsum(
            "tab,tad->tbd", blk_tiles, row_data, preferred_element_type=jnp.float32
        )
        select = (
            (slot_pos[None, :, 1] == tile_ids[:, None]) & (slot_ids[None, :] < live_count)
        ).astype(jnp.float32)
        carried = carried + jnp.einsum("qt,tbd->qbd", select, product, precision=PRECISE)
        if pass_idx > 0:
            carried = shifted(carried.astype(jnp.bfloat16), "blk", -rep_count).astype(carried.dtype)
    for shift_bit in range(rep_bits):
        arrived = shifted(carried.astype(jnp.bfloat16), "blk", -(1 << shift_bit)).astype(
            carried.dtype
        )
        carried = jnp.where(rep_index >> shift_bit & 1 == 1, arrived, carried)
    terms = carried.reshape(rows_blk, feat_width) + self_share
    back_rows = lax.psum_scatter(terms.astype(jnp.bfloat16), "rep", scatter_dimension=0, tiled=True)
    grad_norm = jnp.stack([cot_cent / col_scale, cot_sum, -col_mean * grad_cent_total]) / node_count
    return (normed, back_rows, grad_neigh, grad_norm)


def solution(mesh):
    in_specs = (
        P("blk", None),
        P("blk"),
        P("blk", "rep", None, None, None, None),
        P("blk", "rep", None),
        P("blk", "rep", None, None, None),
        P(),
        P(),
        P("rep"),
        P("rep"),
        P("rep"),
        P("blk", "rep"),
    )
    out_specs = (P("blk", "rep"), P(("blk", "rep"), None), P("blk", "rep"), P(None, "rep"))
    return jax.shard_map(body, mesh=mesh, in_specs=in_specs, out_specs=out_specs, check_vma=False)
```

profile of v0, /device:TPU:1, one launch (start us, length us, event | category | flops | bytes accessed | tf_op | source)
XLA Modules:
  0.0 1051.5 jit_solution(16417494210812277771)
XLA Ops:
  17.0 29.9 %collective-permute-done = bf16[512,1024]{1,0:T(8,128)(2,1)} collective-permute-done((bf16[512,1024]{1,0:T(8,128)(2,1)}, bf16[512,1024]{1,0:T(8,128)(2,1)}, u32[]{:S(2)}, u32[]{:S(2)}) %collective-permute-start) | collective-permute-done | bytes 1048608 | tf_op jit(solution)/shard_map/ppermute | solution.py:12
  49.3 28.7 %collective-permute-done.1 = bf16[512,1024]{1,0:T(8,128)(2,1)} collective-permute-done((bf16[512,1024]{1,0:T(8,128)(2,1)}, bf16[512,1024]{1,0:T(8,128)(2,1)}, u32[]{:S(2)}, u32[]{:S(2)}) %collective-permute-start.1) | collective-permute-done | bytes 1048608 | tf_op jit(solution)/shard_map/ppermute | solution.py:12
  81.6 23.1 %collective-permute-done.2 = bf16[512,1024]{1,0:T(8,128)(2,1)} collective-permute-done((bf16[512,1024]{1,0:T(8,128)(2,1)S(1)}, bf16[512,1024]{1,0:T(8,128)(2,1)}, u32[]{:S(2)}, u32[]{:S(2)}) %collective-permute-start.2) | collective-permute-done | bytes 1048608 | tf_op jit(solution)/shard_map/ppermute | solution.py:12
  108.5 46.0 %collective-permute-done.3 = bf16[512,1024]{1,0:T(8,128)(2,1)} collective-permute-done((bf16[512,1024]{1,0:T(8,128)(2,1)S(1)}, bf16[512,1024]{1,0:T(8,128)(2,1)}, u32[]{:S(2)}, u32[]{:S(2)}) %collective-permute-start.3) | collective-permute-done | bytes 1048608 | tf_op jit(solution)/shard_map/ppermute | solution.py:12
  163.6 5.5 copy.17
  177.0 5.6 copy.18
  182.6 17.5 %collective-permute-done.4 = bf16[512,1024]{1,0:T(8,128)(2,1)} collective-permute-done((bf16[512,1024]{1,0:T(8,128)(2,1)}, bf16[512,1024]{1,0:T(8,128)(2,1)}, u32[]{:S(2)}, u32[]{:S(2)}) %collective-permute-start.4) | collective-permute-done | bytes 1048608 | tf_op jit(solution)/shard_map/ppermute | solution.py:12
  200.1 12.3 %collective-permute-start.5 = (bf16[512,1024]{1,0:T(8,128)(2,1)}, bf16[512,1024]{1,0:T(8,128)(2,1)S(1)}, u32[]{:S(2)}, u32[]{:S(2)}) collective-permute-start(bf16[512,1024]{1,0:T(8,128)(2,1)} %collective-permute-done.4), channel_id=1, source_target_pairs={{0,64},{8,72},{16,80},{24,88},{32,96},{40,104},{48,112},{56,120},{... | collective-permute-start | bytes 3145736 | tf_op jit(solution)/shard_map/ppermute | solution.py:12
  212.4 7.5 fusion.12
  233.4 7.6 fusion.10
  258.5 6.4 fusion.8
  264.9 7.2 add_add_fusion
  274.1 52.1 %all-reduce.5 = bf16[512,1024]{1,0:T(8,128)(2,1)S(1)} all-reduce(f32[512,1024]{1,0:T(8,128)} %bitcast.160), channel_id=1, replica_groups=mesh['blk'=32,'rep'=8] {'rep'}, use_global_device_ids=true, to_apply=%region_0.1 | all-reduce | flops 524288 | bytes 3145728 | tf_op jit(solution)/shard_map/psum | solution.py:71
  327.6 72.8 %psum.43 = f32[128]{0:T(128)} all-reduce(f32[128]{0:T(128)S(1)} %get-tuple-element.43), channel_id=1, replica_groups=mesh['blk'=32,'rep'=8] {'blk'}, use_global_device_ids=true, to_apply=%region_2.3 | all-reduce | flops 128 | bytes 1024 | tf_op jit(solution)/shard_map/psum | solution.py:80
  401.8 56.3 %all-reduce = (f32[128]{0:T(128)S(1)}, f32[128]{0:T(128)S(1)}, f32[128]{0:T(128)S(1)}) all-reduce(f32[128]{0:T(128)} %get-tuple-element.5, f32[128]{0:T(128)} %get-tuple-element.4, f32[128]{0:T(128)} %get-tuple-element.6), channel_id=1, replica_groups=mesh['blk'=32,'rep'=8] {'blk'}, use_global_device_ids=true, to_apply=%region_4.5 | all-reduce | flops 384 | bytes 3072 | tf_op jit(solution)/shard_map/psum | solution.py:82
  463.8 89.9 %all-reduce.4.cloned.1.call-done = bf16[2,256,1024]{2,1,0:T(8,128)(2,1)} async-done(((bf16[2,256,1024]{2,1,0:T(8,128)(2,1)}), bf16[2,256,1024]{2,1,0:T(8,128)(2,1)}) %all-reduce.4.cloned.1.call-update) | async-done | bytes 1048592 | tf_op jit(solution)/shard_map/psum | solution.py:97
  565.2 6.5 fusion.17
  582.7 5.6 copy.22
  588.3 31.6 %collective-permute-done.6 = bf16[2,256,1024]{2,0,1:T(2,128)(2,1)} collective-permute-done((bf16[2,256,1024]{2,0,1:T(2,128)(2,1)S(1)}, bf16[2,256,1024]{2,0,1:T(2,128)(2,1)}, u32[]{:S(2)}, u32[]{:S(2)}) %collective-permute-start.6) | collective-permute-done | bytes 1048608 | tf_op jit(solution)/shard_map/ppermute | solution.py:12
  619.9 8.2 add_convert_fusion.1
  639.1 5.6 copy.23
  644.6 6.2 fusion.2
  650.9 12.3 %collective-permute-done.7 = bf16[2,256,1024]{2,0,1:T(2,128)(2,1)S(1)} collective-permute-done((bf16[2,256,1024]{2,0,1:T(2,128)(2,1)}, bf16[2,256,1024]{2,0,1:T(2,128)(2,1)S(1)}, u32[]{:S(2)}, u32[]{:S(2)}) %collective-permute-start.7) | collective-permute-done | bytes 1048608 | tf_op jit(solution)/shard_map/ppermute | solution.py:12
  672.3 5.5 copy.24
  677.9 16.4 %collective-permute-done.8 = bf16[2,256,1024]{2,0,1:T(2,128)(2,1)S(1)} collective-permute-done((bf16[2,256,1024]{2,0,1:T(2,128)(2,1)}, bf16[2,256,1024]{2,0,1:T(2,128)(2,1)S(1)}, u32[]{:S(2)}, u32[]{:S(2)}) %collective-permute-start.8) | collective-permute-done | bytes 1048608 | tf_op jit(solution)/shard_map/ppermute | solution.py:12
  694.3 7.6 fusion.22
  701.9 14.0 %collective-permute-start.9 = (bf16[2,256,1024]{2,0,1:T(2,128)(2,1)S(1)}, bf16[2,256,1024]{2,0,1:T(2,128)(2,1)S(1)}, u32[]{:S(2)}, u32[]{:S(2)}) collective-permute-start(bf16[2,256,1024]{2,0,1:T(2,128)(2,1)S(1)} %get-tuple-element.45), channel_id=1, source_target_pairs={{0,248},{8,0},{16,8},{24,16},{32,24},{40,32},{48,40},{56,48},{64,5... | collective-permute-start | bytes 3145736 | tf_op jit(solution)/shard_map/ppermute | solution.py:12
  715.9 16.5 %collective-permute-done.9 = bf16[2,256,1024]{2,0,1:T(2,128)(2,1)S(1)} collective-permute-done((bf16[2,256,1024]{2,0,1:T(2,128)(2,1)S(1)}, bf16[2,256,1024]{2,0,1:T(2,128)(2,1)S(1)}, u32[]{:S(2)}, u32[]{:S(2)}) %collective-permute-start.9) | collective-permute-done | bytes 1048608 | tf_op jit(solution)/shard_map/ppermute | solution.py:12
  735.5 20.6 %collective-permute-done.10 = bf16[2,256,1024]{2,0,1:T(2,128)(2,1)S(1)} collective-permute-done((bf16[2,256,1024]{2,0,1:T(2,128)(2,1)S(1)}, bf16[2,256,1024]{2,0,1:T(2,128)(2,1)S(1)}, u32[]{:S(2)}, u32[]{:S(2)}) %collective-permute-start.10) | collective-permute-done | bytes 1048608 | tf_op jit(solution)/shard_map/ppermute | solution.py:12
  759.7 20.8 %collective-permute-done.11 = bf16[2,256,1024]{2,0,1:T(2,128)(2,1)} collective-permute-done((bf16[2,256,1024]{2,0,1:T(2,128)(2,1)}, bf16[2,256,1024]{2,0,1:T(2,128)(2,1)}, u32[]{:S(2)}, u32[]{:S(2)}) %collective-permute-start.11) | collective-permute-done | bytes 1048608 | tf_op jit(solution)/shard_map/ppermute | solution.py:12
  786.2 218.7 %reduce-scatter.5.cloned.1.call-done = bf16[32,128]{1,0:T(8,128)(2,1)} async-done(((bf16[1024,128]{1,0:T(8,128)(2,1)}), bf16[32,128]{1,0:T(8,128)(2,1)}) %reduce-scatter.5.cloned.1.call-update) | async-done | bytes 8208 | tf_op jit(solution)/shard_map/reduce_scatter | solution.py:101
  1006.2 37.6 %reduce-scatter.3.cloned.1.call-done = bf16[64,1024]{1,0:T(8,128)(2,1)} async-done(((bf16[512,1024]{1,0:T(8,128)(2,1)}), bf16[64,1024]{1,0:T(8,128)(2,1)}) %reduce-scatter.3.cloned.1.call-update) | async-done | bytes 131088 | tf_op jit(solution)/shard_map/reduce_scatter | solution.py:128
  (136 shorter events, 133.3 us)
Async XLA Ops:
  8.0 318.2 %copy-start = (bf16[1024,1024]{1,0:T(8,128)(2,1)S(1)}, bf16[1024,1024]{1,0:T(8,128)(2,1)}, u32[]{:S(2)}) copy-start(bf16[1024,1024]{1,0:T(8,128)(2,1)} %param.17) | copy-start | bytes 6291460
  8.0 545.7 %all-reduce.4.cloned.1.call-start = ((), (), s32[]{:S(2)}) async-start(), calls=%async_computation.2 | async-start | bytes 2097152 | tf_op jit(solution)/shard_map/psum | solution.py:97
  14.8 32.1 %collective-permute-start = (bf16[512,1024]{1,0:T(8,128)(2,1)}, bf16[512,1024]{1,0:T(8,128)(2,1)}, u32[]{:S(2)}, u32[]{:S(2)}) collective-permute-start(bf16[512,1024]{1,0:T(8,128)(2,1)} %broadcast_select_fusion), channel_id=1, source_target_pairs={{0,8},{8,16},{16,24},{24,32},{32,40},{40,48},{48,56},{56,64},{64,7... | collective-permute-start | bytes 3145736 | tf_op jit(solution)/shard_map/ppermute | solution.py:12
  49.3 30.2 %copy-start.9 = (s32[1,1,4]{2,1,0:T(1,128)S(1)}, s32[1,1,4]{2,1,0:T(1,128)}, u32[]{:S(2)}) copy-start(s32[1,1,4]{2,1,0:T(1,128)} %param.14) | copy-start | bytes 52
  49.3 32.3 %copy-start.10 = (s32[1,1,4,4,2]{3,4,2,1,0:T(2,128)S(1)}, s32[1,1,4,4,2]{3,4,2,1,0:T(2,128)}, u32[]{:S(2)}) copy-start(s32[1,1,4,4,2]{3,4,2,1,0:T(2,128)} %param.15) | copy-start | bytes 388
  49.3 28.7 %collective-permute-start.1 = (bf16[512,1024]{1,0:T(8,128)(2,1)}, bf16[512,1024]{1,0:T(8,128)(2,1)}, u32[]{:S(2)}, u32[]{:S(2)}) collective-permute-start(bf16[512,1024]{1,0:T(8,128)(2,1)} %broadcast_select_fusion.1), channel_id=1, source_target_pairs={{0,16},{8,24},{16,32},{24,40},{32,48},{40,56},{48,64},{56,72},{64,... | collective-permute-start | bytes 3145736 | tf_op jit(solution)/shard_map/ppermute | solution.py:12
  79.3 25.3 %collective-permute-start.2 = (bf16[512,1024]{1,0:T(8,128)(2,1)S(1)}, bf16[512,1024]{1,0:T(8,128)(2,1)}, u32[]{:S(2)}, u32[]{:S(2)}) collective-permute-start(bf16[512,1024]{1,0:T(8,128)(2,1)S(1)} %broadcast_select_fusion.2), channel_id=1, source_target_pairs={{0,32},{8,40},{16,48},{24,56},{32,64},{40,72},{48,80},{56,88},{64,... | collective-permute-start | bytes 3145736 | tf_op jit(solution)/shard_map/ppermute | solution.py:12
  80.8 177.6 %copy-start.19 = (pred[4]{0:T(512)(128)(4,1)}, pred[4]{0:T(512)(128)(4,1)S(1)}, u32[]{:S(2)}) copy-start(pred[4]{0:T(512)(128)(4,1)S(1)} %iota_compare_fusion) | copy-start | bytes 16
  81.5 151.9 %copy-start.27 = (pred[4]{0:T(512)(128)(4,1)}, pred[4]{0:T(512)(128)(4,1)S(1)}, u32[]{:S(2)}) copy-start(pred[4]{0:T(512)(128)(4,1)S(1)} %iota_compare_fusion.1) | copy-start | bytes 16
  106.0 48.5 %collective-permute-start.3 = (bf16[512,1024]{1,0:T(8,128)(2,1)S(1)}, bf16[512,1024]{1,0:T(8,128)(2,1)}, u32[]{:S(2)}, u32[]{:S(2)}) collective-permute-start(bf16[512,1024]{1,0:T(8,128)(2,1)S(1)} %broadcast_select_fusion.3), channel_id=1, source_target_pairs={{0,64},{8,72},{16,80},{24,88},{32,96},{40,104},{48,112},{56,120},{... | collective-permute-start | bytes 3145736 | tf_op jit(solution)/shard_map/ppermute | solution.py:12
  106.7 105.7 %copy-start.22 = (pred[4]{0:T(512)(128)(4,1)}, pred[4]{0:T(512)(128)(4,1)S(1)}, u32[]{:S(2)}) copy-start(pred[4]{0:T(512)(128)(4,1)S(1)} %iota_compare_fusion.2) | copy-start | bytes 16
  107.4 157.5 %copy-start.24 = (pred[4]{0:T(512)(128)(4,1)}, pred[4]{0:T(512)(128)(4,1)S(1)}, u32[]{:S(2)}) copy-start(pred[4]{0:T(512)(128)(4,1)S(1)} %iota_compare_fusion.3) | copy-start | bytes 16
  154.5 45.6 %collective-permute-start.4 = (bf16[512,1024]{1,0:T(8,128)(2,1)}, bf16[512,1024]{1,0:T(8,128)(2,1)}, u32[]{:S(2)}, u32[]{:S(2)}) collective-permute-start(bf16[512,1024]{1,0:T(8,128)(2,1)} %collective-permute-done.3), channel_id=1, source_target_pairs={{0,64},{8,72},{16,80},{24,88},{32,96},{40,104},{48,112},{56,120},{... | collective-permute-start | bytes 3145736 | tf_op jit(solution)/shard_map/ppermute | solution.py:12
  200.1 46.2 %collective-permute-start.5 = (bf16[512,1024]{1,0:T(8,128)(2,1)}, bf16[512,1024]{1,0:T(8,128)(2,1)S(1)}, u32[]{:S(2)}, u32[]{:S(2)}) collective-permute-start(bf16[512,1024]{1,0:T(8,128)(2,1)} %collective-permute-done.4), channel_id=1, source_target_pairs={{0,64},{8,72},{16,80},{24,88},{32,96},{40,104},{48,112},{56,120},{... | collective-permute-start | bytes 3145736 | tf_op jit(solution)/shard_map/ppermute | solution.py:12
  274.1 127.1 %copy-start.8 = (bf16[512,128]{1,0:T(8,128)(2,1)S(1)}, bf16[512,128]{1,0:T(8,128)(2,1)}, u32[]{:S(2)}) copy-start(bf16[512,128]{1,0:T(8,128)(2,1)} %param.21) | copy-start | bytes 393220
  274.1 184.0 %copy-start.11 = (f32[128]{0:T(128)S(1)}, f32[128]{0:T(128)}, u32[]{:S(2)}) copy-start(f32[128]{0:T(128)} %param.18) | copy-start | bytes 1540
  463.1 541.8 %reduce-scatter.5.cloned.1.call-start = ((), (), s32[]{:S(2)}) async-start(), calls=%async_computation.4 | async-start | bytes 270336 | tf_op jit(solution)/shard_map/reduce_scatter | solution.py:101
  565.2 10.8 %copy-start.14 = (s32[4]{0:T(128)S(1)}, s32[4]{0:T(128)}, u32[]{:S(2)}) copy-start(s32[4]{0:T(128)} %get-tuple-element.49) | copy-start | bytes 52
  565.2 10.8 %copy-start.2 = (bf16[2,256,1024]{2,1,0:T(8,128)(2,1)S(1)}, bf16[2,256,1024]{2,1,0:T(8,128)(2,1)}, u32[]{:S(2)}) copy-start(bf16[2,256,1024]{2,1,0:T(8,128)(2,1)} %all-reduce.4.cloned.1.call-done) | copy-start | bytes 3145732
  571.7 48.2 %collective-permute-start.6 = (bf16[2,256,1024]{2,0,1:T(2,128)(2,1)S(1)}, bf16[2,256,1024]{2,0,1:T(2,128)(2,1)}, u32[]{:S(2)}, u32[]{:S(2)}) collective-permute-start(bf16[2,256,1024]{2,0,1:T(2,128)(2,1)S(1)} %fusion.17), channel_id=1, source_target_pairs={{0,192},{8,200},{16,208},{24,216},{32,224},{40,232},{48,240},{56,2... | collective-permute-start | bytes 3145736 | tf_op jit(solution)/shard_map/ppermute | solution.py:12
  582.7 37.2 %copy-start.26 = (s32[4]{0:T(128)S(1)}, s32[4]{0:T(128)}, u32[]{:S(2)}) copy-start(s32[4]{0:T(128)} %get-tuple-element.50) | copy-start | bytes 52
  582.7 37.2 %copy-start.28 = (pred[4]{0:T(512)(128)(4,1)S(1)}, pred[4]{0:T(512)(128)(4,1)}, u32[]{:S(2)}) copy-start(pred[4]{0:T(512)(128)(4,1)} %copy-done.27) | copy-start | bytes 16
  619.9 12.5 %copy-start.13 = (s32[4]{0:T(128)S(1)}, s32[4]{0:T(128)}, u32[]{:S(2)}) copy-start(s32[4]{0:T(128)} %get-tuple-element.31) | copy-start | bytes 52
  628.1 35.1 %collective-permute-start.7 = (bf16[2,256,1024]{2,0,1:T(2,128)(2,1)}, bf16[2,256,1024]{2,0,1:T(2,128)(2,1)S(1)}, u32[]{:S(2)}, u32[]{:S(2)}) collective-permute-start(bf16[2,256,1024]{2,0,1:T(2,128)(2,1)} %add_convert_fusion.1), channel_id=1, source_target_pairs={{0,192},{8,200},{16,208},{24,216},{32,224},{40,232},{48,240},{56,2... | collective-permute-start | bytes 3145736 | tf_op jit(solution)/shard_map/ppermute | solution.py:12
  650.9 14.8 %copy-start.12 = (s32[4]{0:T(128)S(1)}, s32[4]{0:T(128)}, u32[]{:S(2)}) copy-start(s32[4]{0:T(128)} %get-tuple-element.53) | copy-start | bytes 52
  665.4 28.8 %collective-permute-start.8 = (bf16[2,256,1024]{2,0,1:T(2,128)(2,1)}, bf16[2,256,1024]{2,0,1:T(2,128)(2,1)S(1)}, u32[]{:S(2)}, u32[]{:S(2)}) collective-permute-start(bf16[2,256,1024]{2,0,1:T(2,128)(2,1)} %add_convert_fusion), channel_id=1, source_target_pairs={{0,192},{8,200},{16,208},{24,216},{32,224},{40,232},{48,240},{56,2... | collective-permute-start | bytes 3145736 | tf_op jit(solution)/shard_map/ppermute | solution.py:12
  672.3 22.0 %copy-start.25 = (pred[4]{0:T(512)(128)(4,1)S(1)}, pred[4]{0:T(512)(128)(4,1)}, u32[]{:S(2)}) copy-start(pred[4]{0:T(512)(128)(4,1)} %copy-done.24) | copy-start | bytes 16
  701.9 30.4 %collective-permute-start.9 = (bf16[2,256,1024]{2,0,1:T(2,128)(2,1)S(1)}, bf16[2,256,1024]{2,0,1:T(2,128)(2,1)S(1)}, u32[]{:S(2)}, u32[]{:S(2)}) collective-permute-start(bf16[2,256,1024]{2,0,1:T(2,128)(2,1)S(1)} %get-tuple-element.45), channel_id=1, source_target_pairs={{0,248},{8,0},{16,8},{24,16},{32,24},{40,32},{48,40},{56,48},{64,5... | collective-permute-start | bytes 3145736 | tf_op jit(solution)/shard_map/ppermute | solution.py:12
  735.4 20.7 %collective-permute-start.10 = (bf16[2,256,1024]{2,0,1:T(2,128)(2,1)S(1)}, bf16[2,256,1024]{2,0,1:T(2,128)(2,1)S(1)}, u32[]{:S(2)}, u32[]{:S(2)}) collective-permute-start(bf16[2,256,1024]{2,0,1:T(2,128)(2,1)S(1)} %get-tuple-element.12), channel_id=1, source_target_pairs={{0,240},{8,248},{16,0},{24,8},{32,16},{40,24},{48,32},{56,40},{64,... | collective-permute-start | bytes 3145736 | tf_op jit(solution)/shard_map/ppermute | solution.py:12
  758.2 22.3 %collective-permute-start.11 = (bf16[2,256,1024]{2,0,1:T(2,128)(2,1)}, bf16[2,256,1024]{2,0,1:T(2,128)(2,1)}, u32[]{:S(2)}, u32[]{:S(2)}) collective-permute-start(bf16[2,256,1024]{2,0,1:T(2,128)(2,1)} %fusion.23), channel_id=1, source_target_pairs={{0,224},{8,232},{16,240},{24,248},{32,0},{40,8},{48,16},{56,24},{6... | collective-permute-start | bytes 3145736 | tf_op jit(solution)/shard_map/ppermute | solution.py:12
  759.6 284.2 %reduce-scatter.3.cloned.1.call-start = ((), (), s32[]{:S(2)}) async-start(), calls=%async_computation.3 | async-start | bytes 1179648 | tf_op jit(solution)/shard_map/reduce_scatter | solution.py:128
  782.4 261.3 %copy-start.1 = (bf16[1024,1024]{1,0:T(8,128)(2,1)S(1)}, bf16[1024,1024]{1,0:T(8,128)(2,1)}, u32[]{:S(2)}) copy-start(bf16[1024,1024]{1,0:T(8,128)(2,1)} %param.17) | copy-start | bytes 6291460
  (12 other events, 50.6 us)
Sparse Core Ops, SparseCore 0:
  463.2 90.4 all-reduce.3
Sparse Core Ops, SparseCore 1:
  759.7 245.2 reduce-scatter.4
  1008.0 35.7 reduce-scatter.2
where the time goes:
time: 1060 us; the launch traced here: 1050 us
  waiting for transfers between devices  615 us (58%)
  blocking collectives  181 us (17%)
  matrix products  102 us (10%)
  local copies, waits for them, and re-layouts  70.7 us (7%)
  starting transfers between devices  37.9 us (4%)
  other arithmetic  28.3 us (3%)
  between operations  16.2 us (2%)
    ppermute x12, waiting for transfers between devices, shifted(): return lax.ppermute(x, axis, [(i, (i + by) % size) for i in range(size)])  269 us
    reduce_scatter x1, waiting for transfers between devices, body(): lax.psum_scatter(weight_term.astype(jnp.bfloat16), 'blk', scatter_dimensi...  219 us
    psum x1, waiting for transfers between devices, body(): grad_agg = lax.psum(agg_share.astype(jnp.bfloat16), 'rep')  89.9 us
    psum x1, blocking collectives, body(): col_mean = lax.psum(jnp.sum(pre_norm, axis=0), 'blk') / node_count  72.8 us
    psum x1, blocking collectives, body(): spread = lax.psum(jnp.sum(centered * centered, axis=0), 'blk') / node_count  56.3 us
    psum x1, blocking collectives, body(): agg_rows = lax.psum(partial_value.reshape(rows_blk, feat_width), 'rep')  52.1 us
    ppermute x12, starting transfers between devices, shifted(): return lax.ppermute(x, axis, [(i, (i + by) % size) for i in range(size)])  37.7 us
    reduce_scatter x1, waiting for transfers between devices, body(): lax.psum_scatter(terms.astype(jnp.bfloat16), 'rep', scatter_dimension=0,...  37.6 us
  transfers between devices with their start and end apart: 15, of which 15 were waited for; matrix products, arithmetic and copies ran while one was open for 11% of the time, Pallas kernels for 0%

commit v1 on v0

v1 whole, which is shorter than its diff:
```python
import jax
import jax.numpy as jnp
from jax import lax
from jax.experimental import pallas as pl
from jax.experimental.pallas import tpu as pltpu
from jax.sharding import PartitionSpec as P

EPSILON = 1e-05
MESH = pl.DeviceIdType.MESH
NY = 4
NX = 4
BF16 = jnp.bfloat16
F32 = jnp.float32


def remote(src, dst, send_sem, recv_sem, blk, rep):
    return pltpu.make_async_remote_copy(
        src_ref=src,
        dst_ref=dst,
        send_sem=send_sem,
        recv_sem=recv_sem,
        device_id=(blk, rep),
        device_id_type=MESH,
    )


def greet(peers):
    barrier = pltpu.get_barrier_semaphore()
    for blk, rep in peers:
        pl.semaphore_signal(barrier, inc=1, device_id=(blk, rep), device_id_type=MESH)
    pl.semaphore_wait(barrier, len(peers))


class Place:
    def __init__(self):
        self.b = lax.axis_index("blk")
        self.r = lax.axis_index("rep")
        self.nb = lax.axis_size("blk")
        self.nr = lax.axis_size("rep")
        self.nz = self.nb // NY
        self.y = self.b % NY
        self.z = self.b // NY
        self.x = self.r // 2
        self.k = self.r % 2
        self.sib = self.x * 2 + (1 - self.k)

    def block(self, dy, dz):
        return ((self.z + dz + self.nz) % self.nz) * NY + (self.y + dy + NY) % NY

    def across(self, dx):
        return ((self.x + dx) % NX) * 2 + self.k

    def torus_peers(self):
        steps = ((1, 0), (-1, 0), (0, 1), (0, -1))
        return [(self.block(dy, dz), self.r) for dy, dz in steps]

    def rep_peers(self):
        return [(self.b, (self.r + d) % self.nr) for d in range(1, self.nr)]

    def line_peers(self):
        return [(self.b, self.across(d)) for d in range(1, NX)] + [(self.b, self.sib)]


DYS = (0, -1, 1, 2)


def gather_kernel(
    piece_ref,
    adj_ref,
    agg_ref,
    g,
    o,
    acc,
    pb,
    rb1,
    qb,
    rb2,
    piece_recv,
    half_recv,
    line_send,
    swap_send,
    swap_recv,
    own_sem,
    red_send,
    red_recv1,
    red_recv2,
    all_send,
    all_recv,
    sib_recv,
):
    at = Place()
    b, r, nr = at.b, at.r, at.nr
    rows = piece_ref.shape[0]
    half = rows // 2
    greet(at.torus_peers() + at.rep_peers())
    g[b] = piece_ref[...]

    def to_line(dyi, dz, dz_step):
        c = at.block(DYS[dyi], dz)
        target = (dz - dz_step) % at.nz
        remote(
            g.at[c], g.at[c], line_send, piece_recv.at[dyi, target], at.block(0, dz_step), r
        ).start()

    def hand_out(dyi, dz):
        c = at.block(DYS[dyi], dz)
        diff = (b - c + at.nb) % at.nb
        goal = diff % nr
        step = diff // nr

        @pl.when(goal != r)
        def _():
            remote(
                g.at[c], o.at[step, r], swap_send, swap_recv.at[step], b, goal
            ).start()

        @pl.when(goal == r)
        def _():
            pltpu.make_async_copy(g.at[c], o.at[step, r], own_sem.at[step]).start()

    def arrive(dyi, dz):
        c = at.block(DYS[dyi], dz)
        remote(
            g.at[c], g.at[c], line_send, piece_recv.at[dyi, dz % at.nz], b, r
        ).wait_recv()

    for dyi, dy in ((2, -1), (1, 1)):
        remote(
            g.at[b], g.at[b], line_send, piece_recv.at[1 if dy == 1 else 2, 0], at.block(dy, 0), r
        ).start()
    to_line(0, 0, 1)
    to_line(0, 0, -1)
    hand_out(0, 0)
    for dyi, onward, low in ((1, 1, 0), (2, -1, half)):
        arrive(dyi, 0)
        c = at.block(DYS[dyi], 0)
        part = pl.ds(low, half)
        remote(
            g.at[c, part], g.at[c, part], line_send, half_recv.at[dyi - 1], at.block(onward, 0), r
        ).start()
        to_line(dyi, 0, 1)
        to_line(dyi, 0, -1)
        hand_out(dyi, 0)
    far = at.block(2, 0)
    for i, low in ((0, 0), (1, half)):
        part = pl.ds(low, half)
        remote(
            g.at[far, part], g.at[far, part], line_send, half_recv.at[i], b, r
        ).wait_recv()
    to_line(3, 0, 1)
    to_line(3, 0, -1)
    hand_out(3, 0)
    reach = at.nz // 2
    for t in range(1, reach):
        for dyi in range(4):
            for way in (1, -1):
                dz = -t * way
                arrive(dyi, dz)
                if t < reach - 1 or (way == 1) == (dyi < 2):
                    to_line(dyi, dz, way)
                hand_out(dyi, dz)
    for dyi in (0, 2, 1, 3):
        arrive(dyi, reach)
        hand_out(dyi, reach)

    wide = acc.shape[1]
    tile = 256
    for i, step in enumerate((0, 1, 3, 2)):
        pltpu.make_async_copy(o.at[step, 0], o.at[step, 0], own_sem.at[step]).wait()
        some = o.at[step, pl.ds(0, nr - 1)]
        remote(some, some, swap_send, swap_recv.at[step], b, r).wait_recv()

        def tiles(n, carry, step=step, i=i):
            cols = pl.ds(pl.multiple_of(n * tile, tile), tile)
            source = o[step, :, :, cols].reshape(nr * rows, tile)
            out = jnp.dot(adj_ref[step], source, preferred_element_type=F32)
            acc[:, cols] = out if i == 0 else acc[:, cols] + out
            return carry

        lax.fori_loop(0, wide // tile, tiles, 0)

    x, k, sib = at.x, at.k, at.sib
    for m in range(NX):
        other = (1 - k) * NX + m
        part = acc[pl.ds(pl.multiple_of(other * rows, rows), rows), :]
        pb[m] = part.astype(BF16)
    remote(pb, rb1, red_send.at[0], red_recv1, b, sib).start()
    remote(pb, rb1, red_send.at[0], red_recv1, b, sib).wait_recv()
    for d in (2, 1, 3):
        goal = (x + d) % NX
        mine = k * NX + goal
        part = acc[pl.ds(pl.multiple_of(mine * rows, rows), rows), :]
        qb[d - 1] = (part + rb1[goal].astype(F32)).astype(BF16)
        remote(
            qb.at[d - 1], rb2.at[d - 1], red_send.at[d], red_recv2.at[d - 1], b, at.across(d)
        ).start()
    home = k * NX + x
    total = acc[pl.ds(pl.multiple_of(home * rows, rows), rows), :] + rb1[x].astype(F32)
    for d in (1, 3, 2):
        remote(
            qb.at[d - 1], rb2.at[d - 1], red_send.at[d], red_recv2.at[d - 1], b, at.across(d)
        ).wait_recv()
        total = total + rb2[d - 1].astype(F32)
    agg_ref[home] = total.astype(BF16)
    for d in (2, 1, 3):
        remote(
            agg_ref.at[home], agg_ref.at[home], all_send.at[d - 1], all_recv.at[d - 1], b, at.across(d)
        ).start()
    remote(
        agg_ref.at[home], agg_ref.at[home], all_send.at[3], sib_recv.at[0], b, sib
    ).start()
    for d in (1, 3, 2):
        came = k * NX + (x - d + NX) % NX
        remote(
            agg_ref.at[came], agg_ref.at[came], all_send.at[d - 1], all_recv.at[d - 1], b, sib
        ).wait_recv()
        remote(
            agg_ref.at[came], agg_ref.at[came], all_send.at[3 + d], sib_recv.at[d], b, sib
        ).start()
    for d in range(4):
        came = (1 - k) * NX + (x - d + NX) % NX
        remote(
            agg_ref.at[came], agg_ref.at[came], all_send.at[3], sib_recv.at[d], b, sib
        ).wait_recv()
    count = 3 + 4 * (at.nz - 1)
    some = g.at[pl.ds(0, count)]
    remote(some, some, line_send, piece_recv.at[0, 0], b, sib).wait_send()
    some = g.at[pl.ds(0, 4 * (nr - 1))]
    remote(some, some, swap_send, piece_recv.at[0, 0], b, sib).wait_send()
    remote(pb, rb1, red_send.at[0], red_recv1, b, sib).wait_send()
    for d in range(1, NX):
        remote(
            qb.at[d - 1], rb2.at[d - 1], red_send.at[d], red_recv2.at[d - 1], b, sib
        ).wait_send()
    for i in range(7):
        remote(
            agg_ref.at[home], agg_ref.at[home], all_send.at[i], sib_recv.at[0], b, sib
        ).wait_send()


def gather_features(piece, adj):
    rows, wide = piece.shape
    nb, nr = lax.axis_size("blk"), lax.axis_size("rep")
    dma = pltpu.SemaphoreType.DMA
    vmem = pl.BlockSpec(memory_space=pltpu.VMEM)
    return pl.pallas_call(
        gather_kernel,
        out_shape=jax.ShapeDtypeStruct((nr, rows, wide), BF16),
        in_specs=[vmem, vmem],
        out_specs=vmem,
        scratch_shapes=[
            pltpu.VMEM((nb, rows, wide), BF16),
            pltpu.VMEM((nb // nr, nr, rows, wide), BF16),
            pltpu.VMEM((nr * rows, wide), F32),
            pltpu.VMEM((NX, rows, wide), BF16),
            pltpu.VMEM((NX, rows, wide), BF16),
            pltpu.VMEM((NX - 1, rows, wide), BF16),
            pltpu.VMEM((NX - 1, rows, wide), BF16),
            dma((4, nb // NY)),
            dma((2,)),
            dma(()),
            dma(()),
            dma((4,)),
            dma((4,)),
            dma((4,)),
            dma(()),
            dma((3,)),
            dma((7,)),
            dma((3,)),
            dma((4,)),
        ],
        compiler_params=pltpu.CompilerParams(
            collective_id=0, has_side_effects=True, vmem_limit_bytes=48 << 20
        ),
        name="gather_features",
    )(piece, adj)


def stats_kernel(mine_ref, all_ref, send_sem, recv_sem):
    at = Place()
    b, r, nb = at.b, at.r, at.nb
    greet([((b + d) % nb, r) for d in range(1, nb)])
    for d in range(1, nb):
        remote(mine_ref, all_ref.at[b], send_sem, recv_sem, (b + d) % nb, r).start()
    all_ref[b] = mine_ref[...]
    some = all_ref.at[pl.ds(0, nb - 1)]
    remote(some, some, send_sem, recv_sem, b, at.sib).wait()


def share_stats(mine):
    nb = lax.axis_size("blk")
    vmem = pl.BlockSpec(memory_space=pltpu.VMEM)
    return pl.pallas_call(
        stats_kernel,
        out_shape=jax.ShapeDtypeStruct((nb,) + mine.shape, F32),
        in_specs=[vmem],
        out_specs=vmem,
        scratch_shapes=[pltpu.SemaphoreType.DMA(()), pltpu.SemaphoreType.DMA(())],
        compiler_params=pltpu.CompilerParams(collective_id=1, has_side_effects=True),
        name="share_stats",
    )(mine)


def columns_kernel(mine_ref, all_ref, send_sem, line_recv, sib_recv):
    at = Place()
    b, r, x, k, sib = at.b, at.r, at.x, at.k, at.sib
    width = mine_ref.shape[1]
    greet(at.line_peers())

    def cols(rep):
        return all_ref.at[:, pl.ds(pl.multiple_of(rep * width, width), width)]

    for d in (2, 1, 3):
        remote(mine_ref, cols(r), send_sem.at[d - 1], line_recv.at[d - 1], b, at.across(d)).start()
    remote(mine_ref, cols(r), send_sem.at[3], sib_recv.at[0], b, sib).start()
    all_ref[:, pl.ds(pl.multiple_of(r * width, width), width)] = mine_ref[...]
    for d in (1, 3, 2):
        came = cols(at.across(NX - d))
        remote(came, came, send_sem.at[d - 1], line_recv.at[d - 1], b, sib).wait_recv()
        remote(came, came, send_sem.at[3 + d], sib_recv.at[d], b, sib).start()
    for d in range(4):
        came = cols(((x - d + NX) % NX) * 2 + (1 - k))
        remote(came, came, send_sem.at[3], sib_recv.at[d], b, sib).wait_recv()
    for i in range(7):
        remote(mine_ref, mine_ref, send_sem.at[i], sib_recv.at[0], b, sib).wait_send()


def gather_columns(mine):
    rows, width = mine.shape
    nr = lax.axis_size("rep")
    dma = pltpu.SemaphoreType.DMA
    vmem = pl.BlockSpec(memory_space=pltpu.VMEM)
    return pl.pallas_call(
        columns_kernel,
        out_shape=jax.ShapeDtypeStruct((rows, width * nr), BF16),
        in_specs=[vmem],
        out_specs=vmem,
        scratch_shapes=[dma((7,)), dma((3,)), dma((4,))],
        compiler_params=pltpu.CompilerParams(collective_id=2, has_side_effects=True),
        name="gather_columns",
    )(mine)


def scatter_kernel(
    grad_ref,
    adj_ref,
    self_ref,
    term_ref,
    out_ref,
    weight_ref,
    cb,
    pbuf,
    zr,
    yr,
    yh,
    tr,
    swap_send,
    own_sem,
    part_recv,
    line_send,
    z_recv,
    y_recv,
    h_recv,
    term_send,
    term_recv,
):
    at = Place()
    b, r, nb, nr, nz = at.b, at.r, at.nb, at.nr, at.nz
    rows, wide = out_ref.shape
    half = rows // 2
    greet([((b + d) % nb, r) for d in range(1, nb)] + at.rep_peers())
    for d in range(1, nb):
        goal = (b + d) % nb
        remote(term_ref.at[goal], tr.at[b], term_send, term_recv, goal, r).start()

    tile = 256
    across_rows = (((0,), (0,)), ((), ()))
    for step in (2, 1, 3, 0):

        def tiles(n, carry, step=step):
            cols = pl.ds(pl.multiple_of(n * tile, tile), tile)
            out = lax.dot_general(
                adj_ref[step], grad_ref[:, cols], across_rows, preferred_element_type=F32
            )
            cb[step, :, :, cols] = out.astype(BF16).reshape(nr, rows, tile)
            return carry

        lax.fori_loop(0, wide // tile, tiles, 0)
        c = (b - r - nr * step + 2 * nb) % nb
        pltpu.make_async_copy(cb.at[step, r], pbuf.at[c], own_sem.at[step]).start()
        for d in (1, 7, 2, 6, 3, 5, 4):
            goal = (r + d) % nr
            remote(
                cb.at[step, goal], pbuf.at[c], swap_send, part_recv.at[c], b, goal
            ).start()
    for step in range(4):
        c = (b - r - nr * step + 2 * nb) % nb
        pltpu.make_async_copy(cb.at[step, r], pbuf.at[c], own_sem.at[step]).wait()

    def own(dyi, dz):
        c = at.block(DYS[dyi], dz)

        @pl.when((b - c + nb) % nr != r)
        def _():
            remote(pbuf.at[c], pbuf.at[c], swap_send, part_recv.at[c], b, r).wait_recv()

        return c

    reach = nz // 2
    for t in range(reach, 0, -1):
        for dyi in range(4):
            for wi, way in ((0, 1), (1, -1)):
                first = reach if (way == 1) == (dyi < 2) else reach - 1
                if t > first:
                    continue
                c = own(dyi, t * way)
                if t < first:
                    remote(
                        pbuf.at[c], zr.at[wi, dyi, t], line_send, z_recv.at[wi, dyi, t], b, r
                    ).wait_recv()
                    pbuf[c] = (pbuf[c].astype(F32) + zr[wi, dyi, t].astype(F32)).astype(BF16)
                remote(
                    pbuf.at[c],
                    zr.at[wi, dyi, t - 1],
                    line_send,
                    z_recv.at[wi, dyi, t - 1],
                    at.block(0, way),
                    r,
                ).start()

    def column(dyi):
        c = own(dyi, 0)
        for wi in range(2):
            remote(
                pbuf.at[c], zr.at[wi, dyi, 0], line_send, z_recv.at[wi, dyi, 0], b, r
            ).wait_recv()
        return c, pbuf[c].astype(F32) + zr[0, dyi, 0].astype(F32) + zr[1, dyi, 0].astype(F32)

    c, value = column(3)
    pbuf[c] = value.astype(BF16)
    for i, dy in ((0, 1), (1, -1)):
        part = pl.ds(i * half, half)
        remote(
            pbuf.at[c, part], yh.at[i], line_send, h_recv.at[i], at.block(dy, 0), r
        ).start()
    for i, (dyi, dy) in enumerate(((2, 1), (1, -1))):
        c, value = column(dyi)
        pbuf[c] = value.astype(BF16)
        remote(yh.at[i], yh.at[i], line_send, h_recv.at[i], b, r).wait_recv()
        part = pl.ds(i * half, half)
        pbuf[c, part] = (value[i * half : (i + 1) * half] + yh[i].astype(F32)).astype(BF16)
        remote(pbuf.at[c], yr.at[i], line_send, y_recv.at[i], at.block(dy, 0), r).start()
    c, value = column(0)
    value = value + self_ref[...]
    for i in range(2):
        remote(yr.at[i], yr.at[i], line_send, y_recv.at[i], b, r).wait_recv()
        value = value + yr[i].astype(F32)
    out_ref[...] = value.astype(BF16)

    some = tr.at[pl.ds(0, nb - 1)]
    remote(some, some, term_send, term_recv, b, at.sib).wait()
    tr[b] = term_ref[b]
    weight_ref[...] = jnp.sum(tr[...].astype(F32), axis=0)

    count = 4 * (nz - 1) + 3
    some = pbuf.at[pl.ds(0, count)]
    remote(some, some, line_send, term_recv, b, at.sib).wait_send()
    some = pbuf.at[pl.ds(0, 4 * (nr - 1))]
    remote(some, some, swap_send, term_recv, b, at.sib).wait_send()


def scatter_gradients(grad_agg, adj, self_rows, weight_term):
    rows, wide = self_rows.shape
    nb, nr = lax.axis_size("blk"), lax.axis_size("rep")
    thin, width = weight_term.shape
    terms = weight_term.reshape(nb, thin // nb, width)
    dma = pltpu.SemaphoreType.DMA
    vmem = pl.BlockSpec(memory_space=pltpu.VMEM)
    reach = nb // NY // 2
    return pl.pallas_call(
        scatter_kernel,
        out_shape=(
            jax.ShapeDtypeStruct((rows, wide), BF16),
            jax.ShapeDtypeStruct((thin // nb, width), F32),
        ),
        in_specs=[vmem] * 4,
        out_specs=(vmem, vmem),
        scratch_shapes=[
            pltpu.VMEM((nb // nr, nr, rows, wide), BF16),
            pltpu.VMEM((nb, rows, wide), BF16),
            pltpu.VMEM((2, 4, reach, rows, wide), BF16),
            pltpu.VMEM((2, rows, wide), BF16),
            pltpu.VMEM((2, rows // 2, wide), BF16),
            pltpu.VMEM(terms.shape, BF16),
            dma(()),
            dma((4,)),
            dma((nb,)),
            dma(()),
            dma((2, 4, reach)),
            dma((2,)),
            dma((2,)),
            dma(()),
            dma(()),
        ],
        compiler_params=pltpu.CompilerParams(
            collective_id=3, has_side_effects=True, vmem_limit_bytes=48 << 20
        ),
        name="scatter_gradients",
    )(grad_agg, adj, self_rows, terms)


def dense_blocks(tiles, counts, coords):
    steps, slots, tile, _ = tiles.shape
    slot_ids = jnp.arange(slots, dtype=jnp.int32)
    live = slot_ids[None, :] < counts[:, None]
    picked = []
    for i in range(2):
        row = []
        for j in range(2):
            chosen = live & (coords[..., 0] == i) & (coords[..., 1] == j)
            block = jnp.zeros((steps, tile, tile), BF16)
            for t in range(slots):
                block = jnp.where(chosen[:, t, None, None], tiles[:, t], block)
            row.append(block)
        picked.append(jnp.concatenate(row, axis=2))
    return jnp.concatenate(picked, axis=1)


def body(
    features,
    node_order,
    adj_tiles,
    counts,
    coords,
    w_self,
    w_neigh,
    norm_gain,
    norm_bias,
    mean_scale,
    cotangent,
):
    nb, nr = lax.axis_size("blk"), lax.axis_size("rep")
    rep = lax.axis_index("rep")
    rows_blk, wide = features.shape
    width = cotangent.shape[1]
    nodes = rows_blk * nb
    rows = rows_blk // nr
    adj = dense_blocks(adj_tiles[0, 0], counts.reshape(-1), coords[0, 0])

    ids = jnp.arange(rows_blk, dtype=jnp.int32)
    pick = (node_order[:, None] == ids[None, :]).astype(BF16)
    reordered = jnp.dot(pick, features, preferred_element_type=F32).astype(BF16)
    piece = lax.dynamic_slice_in_dim(reordered, rep * rows, rows, 0)
    aggregate = gather_features(piece, adj).reshape(rows_blk, wide)

    self_cols = lax.dynamic_slice_in_dim(w_self, rep * width, width, 1)
    neigh_cols = lax.dynamic_slice_in_dim(w_neigh, rep * width, width, 1)
    pre_norm = jnp.dot(reordered, self_cols, preferred_element_type=F32) + jnp.dot(
        aggregate, neigh_cols, preferred_element_type=F32
    )
    upstream = cotangent.astype(F32)
    near_mean = jnp.mean(pre_norm, axis=0)
    spread_off = pre_norm - near_mean
    local = jnp.stack(
        [
            near_mean,
            jnp.sum(spread_off * spread_off, axis=0),
            jnp.sum(upstream, axis=0),
            jnp.sum(upstream * spread_off, axis=0),
        ]
    )
    every = share_stats(jnp.concatenate([local, jnp.zeros_like(local)], axis=0))
    means, squares, cots, crosses = (every[:, i] for i in range(4))
    col_mean = jnp.sum(means, axis=0) / nb
    moved = means - mean_scale * col_mean
    spread = jnp.sum(squares + rows_blk * moved * moved, axis=0) / nodes
    cot_sum = jnp.sum(cots, axis=0)
    cot_cent = jnp.sum(crosses + cots * moved, axis=0)

    centered = pre_norm - mean_scale * col_mean
    col_scale = jnp.sqrt(spread + EPSILON)
    normed = (norm_gain * centered / col_scale + norm_bias).astype(BF16)
    grad_centered = norm_gain * upstream / col_scale - centered * (
        norm_gain * cot_cent / (nodes * col_scale**3)
    )
    grad_cent_total = (
        norm_gain * cot_sum / col_scale
        - (1.0 - mean_scale) * col_mean * norm_gain * cot_cent / col_scale**3
    )
    grad_pre = (grad_centered - mean_scale * grad_cent_total / nodes).astype(BF16)

    grad_full = gather_columns(grad_pre)
    by_cols = (((1,), (1,)), ((), ()))
    by_nodes = (((0,), (0,)), ((), ()))
    grad_agg = lax.dot_general(
        grad_full, w_neigh, by_cols, preferred_element_type=F32
    ).astype(BF16)
    own_rows = lax.dynamic_slice_in_dim(grad_full, rep * rows, rows, 0)
    self_rows = lax.dot_general(own_rows, w_self, by_cols, preferred_element_type=F32)
    weight_term = lax.dot_general(
        aggregate, grad_pre, by_nodes, preferred_element_type=F32
    ).astype(BF16)
    grad_feats, weight_sum = scatter_gradients(grad_agg, adj, self_rows, weight_term)
    grad_neigh = weight_sum / nodes
    grad_norm = jnp.stack([cot_cent / col_scale, cot_sum, -col_mean * grad_cent_total]) / nodes
    return (normed, grad_feats, grad_neigh, grad_norm)


def solution(mesh):
    in_specs = (
        P("blk", None),
        P("blk"),
        P("blk", "rep", None, None, None, None),
        P("blk", "rep", None),
        P("blk", "rep", None, None, None),
        P(),
        P(),
        P("rep"),
        P("rep"),
        P("rep"),
        P("blk", "rep"),
    )
    out_specs = (P("blk", "rep"), P(("blk", "rep"), None), P("blk", "rep"), P(None, "rep"))
    return jax.shard_map(body, mesh=mesh, in_specs=in_specs, out_specs=out_specs, check_vma=False)
```

time: 1060 us -> 212 us (0.20)
  waiting for transfers between devices: 615 us -> 0 us
  Pallas kernels: 0 us -> 193 us
  blocking collectives: 181 us -> 0 us
  matrix products: 102 us -> 8.3 us
  local copies, waits for them, and re-layouts: 70.7 us -> 3.4 us
  starting transfers between devices: 37.9 us -> 0 us
  other arithmetic: 28.3 us -> 6.33 us
  between operations: 16.2 us -> 0.87 us
    ppermute x12 -> x0, waiting for transfers between devices: 269 us -> none  [shifted(): return lax.ppermute(x, axis, [(i, (i + by) % size) for i in range(size)])]
    reduce_scatter x2 -> x0, waiting for transfers between devices: 256 us -> none  [the longest x1 219 us: body(): lax.psum_scatter(weight_term.astype(jnp.bfloat16), 'blk', scatter_dimensi...]
    pallas_call x0 -> x4, Pallas kernels: none -> 193 us  [the longest x1 89.4 us: gather_features(): pl.pallas_call(gather_kernel, out_shape=jax.ShapeDtypeStruct((nr, rows, w...]
    psum x3 -> x0, blocking collectives: 181 us -> none  [the longest x1 72.8 us: body(): col_mean = lax.psum(jnp.sum(pre_norm, axis=0), 'blk') / node_count]
    dot_general x21 -> x6, matrix products: 102 us -> 8.3 us  [the longest x1 2.51 us: body(): lax.dot_general(own_rows, w_self, by_cols, preferred_element_type=F32)]
    psum x1 -> x0, waiting for transfers between devices: 89.9 us -> none  [body(): grad_agg = lax.psum(agg_share.astype(jnp.bfloat16), 'rep')]
    dot_general x8 -> x0, local copies, waits for them, and re-layouts: 44.5 us -> none  [the longest x4 22.3 us: body(): jnp.einsum('tab,tbd->tad', gather_blk_tiles, gathered, preferred_element_...]
    ppermute x12 -> x0, starting transfers between devices: 37.7 us -> none  [shifted(): return lax.ppermute(x, axis, [(i, (i + by) % size) for i in range(size)])]
  transfers between devices with their start and end apart: 15 -> 0, of which waited for: 15 -> 0; matrix products, arithmetic and copies ran while one was open for 11% -> 0% of each run, Pallas kernels for 0% -> 0%
where the time goes in v1:
time: 212 us
  Pallas kernels  193 us (91%)
  matrix products  8.3 us (4%)
  other arithmetic  6.33 us (3%)
  local copies, waits for them, and re-layouts  3.4 us (2%)
    pallas_call x1, Pallas kernels, gather_features(): pl.pallas_call(gather_kernel, out_shape=jax.ShapeDtypeStruct((nr, rows, w...  89.4 us
    pallas_call x1, Pallas kernels, scatter_gradients(): pl.pallas_call(scatter_kernel, out_shape=(jax.ShapeDtypeStruct((rows, wid...  78.8 us
    pallas_call x1, Pallas kernels, gather_columns(): pl.pallas_call(columns_kernel, out_shape=jax.ShapeDtypeStruct((rows, widt...  13.8 us
    pallas_call x1, Pallas kernels, share_stats(): pl.pallas_call(stats_kernel, out_shape=jax.ShapeDtypeStruct((nb,) + mine....  10.8 us

profile of v1, /device:TPU:1, one launch (start us, length us, event | category | flops | bytes accessed | tf_op | source)
XLA Modules:
  0.0 211.6 jit_solution(10987442553755184598)
XLA Ops:
  0.6 0.0 copy-start
  0.7 0.8 copy.26
  1.5 0.7 bitcast_and_fusion.3
  2.2 0.7 bitcast_and_fusion.1
  3.0 0.3 slice_reduce_fusion.3
  3.2 0.3 slice_reduce_fusion.7
  3.6 2.1 %convolution_convert_fusion.1 = bf16[512,1024]{1,0:T(8,128)(2,1)S(1)} fusion(bf16[512,1024]{1,0:T(8,128)(2,1)} %param.11, s32[512]{0:T(512)} %param.12), kind=kOutput, calls=%fused_computation.3 | convolution fusion | flops 537657344 | bytes 2099200 | tf_op jit(solution)/shard_map/dot_general | solution.py:552
  5.7 1.4 fusion.6
  7.1 0.2 copy.25
  7.3 0.2 select_select_fusion.2
  7.6 0.2 select_select_fusion.3
  7.8 0.2 maximum_maximum_fusion.adj_ref
  8.0 0.0 copy-start.6
  8.0 89.4 %gather_features.1 = bf16[8,64,1024]{2,1,0:T(8,128)(2,1)S(1)} custom-call(bf16[64,1024]{1,0:T(8,128)(2,1)S(1)} %constant_dynamic-slice_fusion.piece_ref, bf16[4,512,512]{2,1,0:T(8,128)(2,1)S(1)} %maximum_maximum_fusion.adj_ref), custom_call_target="tpu_custom_call" | custom-call | tf_op jit(solution)/shard_map/gather_features/pallas_call | solution.py:246
  97.5 0.0 copy-start.7
  97.5 0.0 copy-start.8
  97.5 0.5 fusion.23
  98.0 0.1 fusion.1
  98.1 0.6 concatenate.15.mine_ref
  98.7 10.8 %share_stats.1 = f32[32,8,128]{2,1,0:T(8,128)} custom-call(f32[8,128]{1,0:T(8,128)} %concatenate.15.mine_ref), custom_call_target="tpu_custom_call" | custom-call | tf_op jit(solution)/shard_map/share_stats/pallas_call | solution.py:293
  109.5 1.2 slice_reduce_fusion.16
  110.8 0.6 maximum_multiply_fusion
  111.4 1.7 fusion.8
  113.0 0.5 convolution_convert_fusion.2
  113.5 0.2 copy-done.5
  113.7 13.8 %gather_columns.1 = bf16[512,1024]{1,0:T(8,128)(2,1)} custom-call(bf16[512,128]{1,0:T(8,128)(2,1)} %copy-done.5), custom_call_target="tpu_custom_call" | custom-call | tf_op jit(solution)/shard_map/gather_columns/pallas_call | solution.py:333
  127.5 2.5 %fusion.9.self_ref = f32[64,1024]{1,0:T(8,128)S(1)} fusion(bf16[1024,1024]{1,0:T(8,128)(2,1)} %param.16, bf16[512,1024]{1,0:T(8,128)(2,1)} %gather_columns.1, s32[]{:T(128)S(6)} %select_n.58), kind=kOutput, calls=%fused_computation.29 | convolution fusion | flops 134217728 | bytes 2490372 | tf_op jit(solution)/shard_map/dot_general | solution.py:599
  130.0 1.3 convolution_convert_fusion.grad_ref
  131.3 0.3 copy-done.2
  131.6 78.8 %scatter_gradients.1 = (bf16[64,1024]{1,0:T(8,128)(2,1)S(1)}, f32[32,128]{1,0:T(8,128)S(1)}) custom-call(bf16[512,1024]{1,0:T(8,128)(2,1)S(1)} %convolution_convert_fusion.grad_ref, bf16[4,512,512]{2,1,0:T(8,128)(2,1)S(1)} %copy-done.2, f32[64,1024]{1,0:T(8,128)S(1)} %fusion.9.self_ref, bf16[32,32,128]{2,1,0:T(8,128)(2,1)S(1)} %bitcast.91), custom_call_target="tpu_custom_call" | custom-call | tf_op jit(solution)/shard_map/scatter_gradients/pallas_call | solution.py:480
  210.4 0.6 broadcast_multiply_fusion
  211.0 0.7 copy.28
  (23 shorter events, 0.1 us)
Async XLA Ops:
  0.6 96.9 %copy-start = (bf16[1024,1024]{1,0:T(8,128)(2,1)S(1)}, bf16[1024,1024]{1,0:T(8,128)(2,1)}, u32[]{:S(2)}) copy-start(bf16[1024,1024]{1,0:T(8,128)(2,1)} %param.17) | copy-start | bytes 6291460
  3.5 3.6 %copy-start.3 = (bf16[1,1,4,4,256,256]{5,4,3,2,1,0:T(8,128)(2,1)S(1)}, bf16[1,1,4,4,256,256]{5,4,3,2,1,0:T(8,128)(2,1)}, u32[]{:S(2)}) copy-start(bf16[1,1,4,4,256,256]{5,4,3,2,1,0:T(8,128)(2,1)} %param.13) | copy-start | bytes 6291460
  8.0 90.0 %copy-start.1 = (bf16[4,512,512]{2,1,0:T(8,128)(2,1)}, bf16[4,512,512]{2,1,0:T(8,128)(2,1)S(1)}, u32[]{:S(2)}) copy-start(bf16[4,512,512]{2,1,0:T(8,128)(2,1)S(1)} %maximum_maximum_fusion.adj_ref) | copy-start | bytes 6291460
  8.0 90.0 %copy-start.6 = (bf16[512,128]{1,0:T(8,128)(2,1)S(1)}, bf16[512,128]{1,0:T(8,128)(2,1)}, u32[]{:S(2)}) copy-start(bf16[512,128]{1,0:T(8,128)(2,1)} %param.21) | copy-start | bytes 393220
  97.5 13.2 %copy-start.9 = (f32[128]{0:T(128)S(1)}, f32[128]{0:T(128)}, u32[]{:S(2)}) copy-start(f32[128]{0:T(128)} %param.20) | copy-start | bytes 1540
  97.5 13.3 %copy-start.7 = (f32[128]{0:T(128)S(1)}, f32[128]{0:T(128)}, u32[]{:S(2)}) copy-start(f32[128]{0:T(128)} %param.18) | copy-start | bytes 1540
  97.5 13.9 %copy-start.8 = (f32[128]{0:T(128)S(1)}, f32[128]{0:T(128)}, u32[]{:S(2)}) copy-start(f32[128]{0:T(128)} %param.19) | copy-start | bytes 1540
  113.0 0.7 copy-start.5
  127.5 2.5 %copy-start.4 = (bf16[512,1024]{1,0:T(8,128)(2,1)S(1)}, bf16[512,1024]{1,0:T(8,128)(2,1)}, u32[]{:S(2)}) copy-start(bf16[512,1024]{1,0:T(8,128)(2,1)} %gather_columns.1) | copy-start | bytes 3145732
  130.0 1.6 copy-start.2

commit v2 on v0

v2 whole, which is shorter than its diff:
```python
import jax
import jax.numpy as jnp
from jax import lax
from jax.experimental import pallas as pl
from jax.experimental.pallas import tpu as pltpu
from jax.sharding import PartitionSpec as P

EPSILON = 1e-05
MESH = pl.DeviceIdType.MESH
NY = 4
NX = 4
BF16 = jnp.bfloat16
F32 = jnp.float32


def remote(src, dst, send_sem, recv_sem, blk, rep):
    return pltpu.make_async_remote_copy(
        src_ref=src,
        dst_ref=dst,
        send_sem=send_sem,
        recv_sem=recv_sem,
        device_id=(blk, rep),
        device_id_type=MESH,
    )


def greet(peers):
    barrier = pltpu.get_barrier_semaphore()
    for blk, rep in peers:
        pl.semaphore_signal(barrier, inc=1, device_id=(blk, rep), device_id_type=MESH)
    pl.semaphore_wait(barrier, len(peers))


class Place:
    def __init__(self):
        self.b = lax.axis_index("blk")
        self.r = lax.axis_index("rep")
        self.nb = lax.axis_size("blk")
        self.nr = lax.axis_size("rep")
        self.nz = self.nb // NY
        self.y = self.b % NY
        self.z = self.b // NY
        self.x = self.r // 2
        self.k = self.r % 2
        self.sib = self.x * 2 + (1 - self.k)

    def block(self, dy, dz):
        return ((self.z + dz + self.nz) % self.nz) * NY + (self.y + dy + NY) % NY

    def across(self, dx):
        return ((self.x + dx) % NX) * 2 + self.k

    def torus_peers(self):
        steps = ((1, 0), (-1, 0), (0, 1), (0, -1))
        return [(self.block(dy, dz), self.r) for dy, dz in steps]

    def rep_peers(self):
        return [(self.b, (self.r + d) % self.nr) for d in range(1, self.nr)]

    def line_peers(self):
        return [(self.b, self.across(d)) for d in range(1, NX)] + [(self.b, self.sib)]


DYS = (0, -1, 1, 2)
ROW_TILE = 128
COL_TILE = 256
BY_FIRST = (((0,), (0,)), ((), ()))
BY_LAST = (((1,), (1,)), ((), ()))


def layer_kernel(
    feat_hbm,
    order_ref,
    tiles_hbm,
    counts_ref,
    coords_ref,
    self_hbm,
    neigh_hbm,
    gain_ref,
    bias_ref,
    scale_ref,
    cot_ref,
    normed_ref,
    out_ref,
    weight_ref,
    norm_ref,
    feat,
    tiles,
    w_self,
    w_neigh,
    load_sem,
    reordered,
    adj,
    self_pre,
    g,
    o,
    acc,
    pb,
    rb1,
    qb,
    rb2,
    agg,
    prod,
    prod_in,
    pre,
    stat,
    stats,
    grad_pre,
    grad_all,
    grad_agg,
    self_rows,
    term,
    term_in,
    cb,
    pbuf,
    zr,
    yr,
    yh,
    piece_recv,
    half_recv,
    line_send,
    swap_send,
    swap_recv,
    own_sem,
    red_send,
    red_recv1,
    red_recv2,
    prod_send,
    prod_recv,
    agg_send,
    agg_recv,
    agg_sib,
    stat_send,
    stat_recv,
    col_send,
    col_recv,
    col_sib,
    term_send,
    term_recv,
    back_own,
    back_send,
    part_recv,
    back_line,
    z_recv,
    y_recv,
    h_recv,
):
    at = Place()
    b, r, nb, nr, nz = at.b, at.r, at.nb, at.nr, at.nz
    x, k, sib = at.x, at.k, at.sib
    rows, wide = out_ref.shape
    half = rows // 2
    rows_blk = rows * nr
    width = cot_ref.shape[1]
    nodes = rows_blk * nb
    reach = nz // 2
    sides = rows_blk // tiles.shape[-1]
    side = tiles.shape[-1]
    slots = tiles.shape[1]

    loads = [
        pltpu.make_async_copy(src, dst, load_sem.at[i])
        for i, (src, dst) in enumerate(
            ((feat_hbm, feat), (tiles_hbm, tiles), (self_hbm, w_self), (neigh_hbm, w_neigh))
        )
    ]
    for load in loads:
        load.start()

    def reorder(low):
        ids = lax.broadcasted_iota(jnp.int32, (rows_blk, ROW_TILE), 0)
        want = order_ref[:, pl.ds(pl.multiple_of(low, ROW_TILE), ROW_TILE)]
        pick = jnp.where(ids == want, 1.0, 0.0).astype(BF16)
        return lax.dot_general(pick, feat[...], BY_FIRST, preferred_element_type=F32).astype(BF16)

    greet([((b + d) % nb, r) for d in range(1, nb)] + at.rep_peers())
    loads[0].wait()
    reordered[x] = reorder(x * ROW_TILE)
    g[b] = reordered[x, pl.ds(pl.multiple_of(k * rows, rows), rows), :]

    def to_line(dyi, dz, dz_step):
        c = at.block(DYS[dyi], dz)
        target = (dz - dz_step) % nz
        remote(
            g.at[c], g.at[c], line_send, piece_recv.at[dyi, target], at.block(0, dz_step), r
        ).start()

    def hand_out(dyi, dz):
        c = at.block(DYS[dyi], dz)
        diff = (b - c + nb) % nb
        goal = diff % nr
        step = diff // nr

        @pl.when(goal != r)
        def _():
            remote(
                g.at[c], o.at[step, r], swap_send, swap_recv.at[step], b, goal
            ).start()

        @pl.when(goal == r)
        def _():
            pltpu.make_async_copy(g.at[c], o.at[step, r], own_sem.at[step]).start()

    def arrive(dyi, dz):
        c = at.block(DYS[dyi], dz)
        remote(
            g.at[c], g.at[c], line_send, piece_recv.at[dyi, dz % nz], b, r
        ).wait_recv()

    def fill_block(step):
        def run():
            if step == 0:
                loads[1].wait()
            for i in range(sides):
                for j in range(sides):
                    block = jnp.zeros((side, side), F32)
                    for t in range(slots):
                        live = (
                            (t < counts_ref[step])
                            & (coords_ref[step, t, 0] == i)
                            & (coords_ref[step, t, 1] == j)
                        )
                        chosen = jnp.where(live, 1.0, 0.0)
                        block = block + chosen * tiles[step, t].astype(F32)
                    adj[step, i * side : (i + 1) * side, j * side : (j + 1) * side] = block.astype(BF16)

        return run

    def fill_rows(d):
        def run():
            n = (x + d) % NX
            if d:
                reordered[n] = reorder(n * ROW_TILE)
            if d == 0:
                loads[2].wait()
            cols = pl.ds(pl.multiple_of(r * width, width), width)
            self_pre[n] = jnp.dot(reordered[n], w_self[:, cols], preferred_element_type=F32)

        return run

    work = [fill_block(step) for step in range(nb // nr)] + [fill_rows(d) for d in range(NX)]

    for dyi, dy in ((2, -1), (1, 1)):
        remote(
            g.at[b], g.at[b], line_send, piece_recv.at[dyi, 0], at.block(dy, 0), r
        ).start()
    to_line(0, 0, 1)
    to_line(0, 0, -1)
    hand_out(0, 0)
    for dyi, onward, low in ((1, 1, 0), (2, -1, half)):
        arrive(dyi, 0)
        c = at.block(DYS[dyi], 0)
        part = pl.ds(low, half)
        remote(
            g.at[c, part], g.at[c, part], line_send, half_recv.at[dyi - 1], at.block(onward, 0), r
        ).start()
        to_line(dyi, 0, 1)
        to_line(dyi, 0, -1)
        hand_out(dyi, 0)
    far = at.block(2, 0)
    for i, low in ((0, 0), (1, half)):
        part = pl.ds(low, half)
        remote(
            g.at[far, part], g.at[far, part], line_send, half_recv.at[i], b, r
        ).wait_recv()
    to_line(3, 0, 1)
    to_line(3, 0, -1)
    hand_out(3, 0)
    for t in range(1, reach):
        for dyi in range(4):
            for way in (1, -1):
                dz = -t * way
                arrive(dyi, dz)
                if t < reach - 1 or (way == 1) == (dyi < 2):
                    to_line(dyi, dz, way)
                hand_out(dyi, dz)
            if work:
                work.pop(0)()
    for dyi in (0, 2, 1, 3):
        arrive(dyi, reach)
        hand_out(dyi, reach)

    for i, step in enumerate((0, 1, 3, 2)):
        pltpu.make_async_copy(o.at[step, 0], o.at[step, 0], own_sem.at[step]).wait()
        some = o.at[step, pl.ds(0, nr - 1)]
        remote(some, some, swap_send, swap_recv.at[step], b, r).wait_recv()

        def part_tile(n, carry, step=step, i=i):
            cols = pl.ds(pl.multiple_of(n * COL_TILE, COL_TILE), COL_TILE)
            source = o[step, :, :, cols].reshape(rows_blk, COL_TILE)
            out = jnp.dot(adj[step], source, preferred_element_type=F32)
            acc[:, cols] = out if i == 0 else acc[:, cols] + out
            return carry

        lax.fori_loop(0, wide // COL_TILE, part_tile, 0)

    def chunk(m):
        return acc[pl.ds(pl.multiple_of(m * rows, rows), rows), :]

    for m in range(NX):
        pb[m] = chunk((1 - k) * NX + m).astype(BF16)
    swap_halves = remote(pb, rb1, red_send.at[0], red_recv1, b, sib)
    swap_halves.start()
    loads[3].wait()
    swap_halves.wait_recv()

    def reduced(d):
        return remote(
            qb.at[d - 1], rb2.at[d - 1], red_send.at[d], red_recv2.at[d - 1], b, at.across(d)
        )

    for d in (2, 1, 3):
        goal = (x + d) % NX
        qb[d - 1] = (chunk(k * NX + goal) + rb1[goal].astype(F32)).astype(BF16)
        reduced(d).start()
    home = k * NX + x
    total = chunk(home) + rb1[x].astype(F32)
    for d in (1, 3, 2):
        reduced(d).wait_recv()
        total = total + rb2[d - 1].astype(F32)
    agg[home] = total.astype(BF16)

    for n in range(wide // COL_TILE):
        cols = slice(n * COL_TILE, (n + 1) * COL_TILE)
        out = jnp.dot(agg[home], w_neigh[:, cols], preferred_element_type=F32)
        for j in range(COL_TILE // width):
            prod[n * (COL_TILE // width) + j] = out[:, j * width : (j + 1) * width]
    for d in (4, 5, 2, 3, 6, 7, 1):
        goal = (r + d) % nr
        remote(prod.at[goal], prod_in.at[home], prod_send, prod_recv, b, goal).start()
    prod_in[home] = prod[r]

    def agg_line(d):
        return remote(
            agg.at[home], agg.at[home], agg_send.at[d - 1], agg_recv.at[d - 1], b, at.across(d)
        )

    for d in (2, 1, 3):
        agg_line(d).start()
    remote(agg.at[home], agg.at[home], agg_send.at[3], agg_sib.at[0], b, sib).start()
    some = prod_in.at[pl.ds(0, nr - 1)]
    remote(some, some, prod_send, prod_recv, b, sib).wait_recv()

    pre[...] = self_pre[...].reshape(rows_blk, width) + prod_in[...].reshape(rows_blk, width)
    upstream = cot_ref[...].astype(F32)
    near_mean = jnp.sum(pre[...], axis=0, keepdims=True) / rows_blk
    off = pre[...] - near_mean
    stat[0:1, :] = near_mean
    stat[1:2, :] = jnp.sum(off * off, axis=0, keepdims=True)
    stat[2:3, :] = jnp.sum(upstream, axis=0, keepdims=True)
    stat[3:4, :] = jnp.sum(upstream * off, axis=0, keepdims=True)
    stat[4:8, :] = jnp.zeros((4, width), F32)
    for d in range(1, nb):
        remote(stat, stats.at[b], stat_send, stat_recv, (b + d) % nb, r).start()
    stats[b] = stat[...]
    some = stats.at[pl.ds(0, nb - 1)]
    remote(some, some, stat_send, stat_recv, b, sib).wait_recv()

    gain, mean_scale = gain_ref[...], scale_ref[...]
    means, cots = stats[:, 0, :], stats[:, 2, :]
    col_mean = jnp.sum(means, axis=0, keepdims=True) / nb
    moved = means - mean_scale * col_mean
    spread = (
        jnp.sum(stats[:, 1, :] + rows_blk * moved * moved, axis=0, keepdims=True) / nodes
    )
    cot_sum = jnp.sum(cots, axis=0, keepdims=True)
    cot_cent = jnp.sum(stats[:, 3, :] + cots * moved, axis=0, keepdims=True)
    col_scale = jnp.sqrt(spread + EPSILON)
    cube = col_scale * col_scale * col_scale
    sharp = gain / col_scale
    weight = gain * cot_cent / (nodes * cube)
    grad_cent_total = sharp * cot_sum - (1.0 - mean_scale) * col_mean * gain * cot_cent / cube
    centered = pre[...] - mean_scale * col_mean
    grad_pre[...] = (
        sharp * upstream - centered * weight - mean_scale * grad_cent_total / nodes
    ).astype(BF16)

    def columns(rep):
        return grad_all.at[:, pl.ds(pl.multiple_of(rep * width, width), width)]

    for d in (2, 1, 3):
        remote(
            grad_pre, columns(r), col_send.at[d - 1], col_recv.at[d - 1], b, at.across(d)
        ).start()
    remote(grad_pre, columns(r), col_send.at[3], col_sib.at[0], b, sib).start()
    grad_all[:, pl.ds(pl.multiple_of(r * width, width), width)] = grad_pre[...]
    normed_ref[...] = (sharp * centered + bias_ref[...]).astype(BF16)
    norm_ref[0:1, :] = cot_cent / col_scale / nodes
    norm_ref[1:2, :] = cot_sum / nodes
    norm_ref[2:3, :] = -col_mean * grad_cent_total / nodes
    for d in (1, 3, 2):
        came = k * NX + (x - d + NX) % NX
        remote(
            agg.at[came], agg.at[came], agg_send.at[d - 1], agg_recv.at[d - 1], b, sib
        ).wait_recv()
        remote(agg.at[came], agg.at[came], agg_send.at[3 + d], agg_sib.at[d], b, sib).start()
    for d in (1, 3, 2):
        came = columns(at.across(NX - d))
        remote(came, came, col_send.at[d - 1], col_recv.at[d - 1], b, sib).wait_recv()
        remote(came, came, col_send.at[3 + d], col_sib.at[d], b, sib).start()
    for d in range(4):
        came = columns(((x - d + NX) % NX) * 2 + (1 - k))
        remote(came, came, col_send.at[3], col_sib.at[d], b, sib).wait_recv()

    def agg_tile(n, carry):
        low = pl.ds(pl.multiple_of(n * COL_TILE, COL_TILE), COL_TILE)
        out = lax.dot_general(
            grad_all[...], w_neigh[low, :], BY_LAST, preferred_element_type=F32
        )
        grad_agg[:, low] = out.astype(BF16)
        return carry

    lax.fori_loop(0, wide // COL_TILE, agg_tile, 0)

    for step in (2, 1, 3, 0):

        def back_tile(n, carry, step=step):
            cols = pl.ds(pl.multiple_of(n * COL_TILE, COL_TILE), COL_TILE)
            out = lax.dot_general(
                adj[step], grad_agg[:, cols], BY_FIRST, preferred_element_type=F32
            )
            cb[step, :, :, cols] = out.astype(BF16).reshape(nr, rows, COL_TILE)
            return carry

        lax.fori_loop(0, wide // COL_TILE, back_tile, 0)
        c = (b - r - nr * step + 2 * nb) % nb
        pltpu.make_async_copy(cb.at[step, r], pbuf.at[c], back_own.at[step]).start()
        for d in (1, 7, 2, 6, 3, 5, 4):
            goal = (r + d) % nr
            remote(
                cb.at[step, goal], pbuf.at[c], back_send, part_recv.at[c], b, goal
            ).start()
    for d in range(4):
        came = (1 - k) * NX + (x - d + NX) % NX
        remote(agg.at[came], agg.at[came], agg_send.at[3], agg_sib.at[d], b, sib).wait_recv()
    thin = weight_ref.shape[0]
    for n in range(wide // COL_TILE):
        cols = slice(n * COL_TILE, (n + 1) * COL_TILE)
        source = agg[:, :, cols].reshape(rows_blk, COL_TILE)
        out = lax.dot_general(source, grad_pre[...], BY_FIRST, preferred_element_type=F32)
        each = COL_TILE // thin
        term[n * each : (n + 1) * each] = out.astype(BF16).reshape(each, thin, width)
    for d in range(1, nb):
        goal = (b + d) % nb
        remote(term.at[goal], term_in.at[b], term_send, term_recv, goal, r).start()
    term_in[b] = term[b]
    own_rows = pl.ds(pl.multiple_of(r * rows, rows), rows)
    self_rows[...] = lax.dot_general(
        grad_all[own_rows, :], w_self[...], BY_LAST, preferred_element_type=F32
    )
    for step in range(4):
        c = (b - r - nr * step + 2 * nb) % nb
        pltpu.make_async_copy(cb.at[step, r], pbuf.at[c], back_own.at[step]).wait()

    def own(dyi, dz):
        c = at.block(DYS[dyi], dz)

        @pl.when((b - c + nb) % nr != r)
        def _():
            remote(pbuf.at[c], pbuf.at[c], back_send, part_recv.at[c], b, r).wait_recv()

        return c

    for t in range(reach, 0, -1):
        for dyi in range(4):
            for wi, way in ((0, 1), (1, -1)):
                first = reach if (way == 1) == (dyi < 2) else reach - 1
                if t > first:
                    continue
                c = own(dyi, t * way)
                if t < first:
                    remote(
                        pbuf.at[c], zr.at[wi, dyi, t], back_line, z_recv.at[wi, dyi, t], b, r
                    ).wait_recv()
                    pbuf[c] = (pbuf[c].astype(F32) + zr[wi, dyi, t].astype(F32)).astype(BF16)
                remote(
                    pbuf.at[c],
                    zr.at[wi, dyi, t - 1],
                    back_line,
                    z_recv.at[wi, dyi, t - 1],
                    at.block(0, way),
                    r,
                ).start()

    def column(dyi):
        c = own(dyi, 0)
        for wi in range(2):
            remote(
                pbuf.at[c], zr.at[wi, dyi, 0], back_line, z_recv.at[wi, dyi, 0], b, r
            ).wait_recv()
        return c, pbuf[c].astype(F32) + zr[0, dyi, 0].astype(F32) + zr[1, dyi, 0].astype(F32)

    c, value = column(3)
    pbuf[c] = value.astype(BF16)
    for i, dy in ((0, 1), (1, -1)):
        part = pl.ds(i * half, half)
        remote(
            pbuf.at[c, part], yh.at[i], back_line, h_recv.at[i], at.block(dy, 0), r
        ).start()
    for i, (dyi, dy) in enumerate(((2, 1), (1, -1))):
        c, value = column(dyi)
        pbuf[c] = value.astype(BF16)
        remote(yh.at[i], yh.at[i], back_line, h_recv.at[i], b, r).wait_recv()
        part = pl.ds(i * half, half)
        pbuf[c, part] = (value[i * half : (i + 1) * half] + yh[i].astype(F32)).astype(BF16)
        remote(pbuf.at[c], yr.at[i], back_line, y_recv.at[i], at.block(dy, 0), r).start()
    c, value = column(0)
    value = value + self_rows[...]
    for i in range(2):
        remote(yr.at[i], yr.at[i], back_line, y_recv.at[i], b, r).wait_recv()
        value = value + yr[i].astype(F32)
    out_ref[...] = value.astype(BF16)

    some = term_in.at[pl.ds(0, nb - 1)]
    remote(some, some, term_send, term_recv, b, sib).wait()
    weight_ref[...] = jnp.sum(term_in[...].astype(F32), axis=0) / nodes

    def sent(some, sem):
        remote(some, some, sem, term_recv, b, sib).wait_send()

    sent(g.at[pl.ds(0, 3 + 4 * (nz - 1))], line_send)
    sent(g.at[pl.ds(0, 4 * (nr - 1))], swap_send)
    sent(pbuf.at[pl.ds(0, 3 + 4 * (nz - 1))], back_line)
    sent(pbuf.at[pl.ds(0, 4 * (nr - 1))], back_send)
    sent(pb, red_send.at[0])
    for d in range(1, NX):
        sent(qb.at[d - 1], red_send.at[d])
    for i in range(7):
        sent(agg.at[0], agg_send.at[i])
        sent(grad_pre, col_send.at[i])
    sent(prod_in.at[pl.ds(0, nr - 1)], prod_send)
    sent(stats.at[pl.ds(0, nb - 1)], stat_send)


def body(
    features,
    node_order,
    adj_tiles,
    counts,
    coords,
    w_self,
    w_neigh,
    norm_gain,
    norm_bias,
    mean_scale,
    cotangent,
):
    nb, nr = lax.axis_size("blk"), lax.axis_size("rep")
    rows_blk, wide = features.shape
    width = cotangent.shape[1]
    rows = rows_blk // nr
    thin = wide // nb
    steps = nb // nr
    reach = nb // NY // 2
    tiles = adj_tiles[0, 0]
    dma = pltpu.SemaphoreType.DMA
    vmem = pl.BlockSpec(memory_space=pltpu.VMEM)
    smem = pl.BlockSpec(memory_space=pltpu.SMEM)
    hbm = pl.BlockSpec(memory_space=pl.ANY)

    def room(*shape, dtype=BF16):
        return pltpu.VMEM(shape, dtype)

    return tuple(
        pl.pallas_call(
            layer_kernel,
            out_shape=(
                jax.ShapeDtypeStruct((rows_blk, width), BF16),
                jax.ShapeDtypeStruct((rows, wide), BF16),
                jax.ShapeDtypeStruct((thin, width), F32),
                jax.ShapeDtypeStruct((3, width), F32),
            ),
            in_specs=[hbm, vmem, hbm, smem, smem, hbm, hbm, vmem, vmem, vmem, vmem],
            out_specs=(vmem,) * 4,
            scratch_shapes=[
                room(rows_blk, wide),
                room(*tiles.shape),
                room(wide, wide),
                room(wide, wide),
                dma((4,)),
                room(NX, ROW_TILE, wide),
                room(steps, rows_blk, rows_blk),
                room(NX, ROW_TILE, width, dtype=F32),
                room(nb, rows, wide),
                room(steps, nr, rows, wide),
                room(rows_blk, wide, dtype=F32),
                room(NX, rows, wide),
                room(NX, rows, wide),
                room(NX - 1, rows, wide),
                room(NX - 1, rows, wide),
                room(nr, rows, wide),
                room(nr, rows, width, dtype=F32),
                room(nr, rows, width, dtype=F32),
                room(rows_blk, width, dtype=F32),
                room(8, width, dtype=F32),
                room(nb, 8, width, dtype=F32),
                room(rows_blk, width),
                room(rows_blk, wide),
                room(rows_blk, wide),
                room(rows, wide, dtype=F32),
                room(nb, thin, width),
                room(nb, thin, width),
                room(steps, nr, rows, wide),
                room(nb, rows, wide),
                room(2, 4, reach, rows, wide),
                room(2, rows, wide),
                room(2, rows // 2, wide),
                dma((4, nb // NY)),
                dma((2,)),
                dma(()),
                dma(()),
                dma((steps,)),
                dma((steps,)),
                dma((4,)),
                dma(()),
                dma((3,)),
                dma(()),
                dma(()),
                dma((7,)),
                dma((3,)),
                dma((4,)),
                dma(()),
                dma(()),
                dma((7,)),
                dma((3,)),
                dma((4,)),
                dma(()),
                dma(()),
                dma((steps,)),
                dma(()),
                dma((nb,)),
                dma(()),
                dma((2, 4, reach)),
                dma((2,)),
                dma((2,)),
            ],
            compiler_params=pltpu.CompilerParams(
                collective_id=0, has_side_effects=True, vmem_limit_bytes=56 << 20
            ),
            name="layer",
        )(
            features,
            node_order.reshape(1, rows_blk),
            tiles,
            counts.reshape(steps),
            coords[0, 0],
            w_self,
            w_neigh,
            norm_gain.reshape(1, width),
            norm_bias.reshape(1, width),
            mean_scale.reshape(1, width),
            cotangent,
        )
    )


def solution(mesh):
    in_specs = (
        P("blk", None),
        P("blk"),
        P("blk", "rep", None, None, None, None),
        P("blk", "rep", None),
        P("blk", "rep", None, None, None),
        P(),
        P(),
        P("rep"),
        P("rep"),
        P("rep"),
        P("blk", "rep"),
    )
    out_specs = (P("blk", "rep"), P(("blk", "rep"), None), P("blk", "rep"), P(None, "rep"))
    return jax.shard_map(body, mesh=mesh, in_specs=in_specs, out_specs=out_specs, check_vma=False)
```

time: 1060 us -> 189 us (0.18)
  waiting for transfers between devices: 615 us -> 0 us
  Pallas kernels: 0 us -> 181 us
  blocking collectives: 181 us -> 0 us
  matrix products: 102 us -> 0 us
  local copies, waits for them, and re-layouts: 70.7 us -> 7.1 us
  starting transfers between devices: 37.9 us -> 0 us
  other arithmetic: 28.3 us -> 0 us
  between operations: 16.2 us -> 0.64 us
    ppermute x12 -> x0, waiting for transfers between devices: 269 us -> none  [shifted(): return lax.ppermute(x, axis, [(i, (i + by) % size) for i in range(size)])]
    reduce_scatter x2 -> x0, waiting for transfers between devices: 256 us -> none  [the longest x1 219 us: body(): lax.psum_scatter(weight_term.astype(jnp.bfloat16), 'blk', scatter_dimensi...]
    psum x3 -> x0, blocking collectives: 181 us -> none  [the longest x1 72.8 us: body(): col_mean = lax.psum(jnp.sum(pre_norm, axis=0), 'blk') / node_count]
    pallas_call x0 -> x1, Pallas kernels: none -> 181 us  [body(): pl.pallas_call(layer_kernel, out_shape=(jax.ShapeDtypeStruct((rows_blk, w...]
    dot_general x21 -> x0, matrix products: 102 us -> none  [the longest x4 28.7 us: body(): jnp.einsum('qt,tad->qad', gather_select, gather_product, precision=PRECISE)]
    psum x1 -> x0, waiting for transfers between devices: 89.9 us -> none  [body(): grad_agg = lax.psum(agg_share.astype(jnp.bfloat16), 'rep')]
    dot_general x8 -> x0, local copies, waits for them, and re-layouts: 44.5 us -> none  [the longest x4 22.3 us: body(): jnp.einsum('tab,tbd->tad', gather_blk_tiles, gathered, preferred_element_...]
    ppermute x12 -> x0, starting transfers between devices: 37.7 us -> none  [shifted(): return lax.ppermute(x, axis, [(i, (i + by) % size) for i in range(size)])]
  transfers between devices with their start and end apart: 15 -> 0, of which waited for: 15 -> 0; matrix products, arithmetic and copies ran while one was open for 11% -> 0% of each run, Pallas kernels for 0% -> 0%
where the time goes in v2:
time: 189 us
  Pallas kernels  181 us (96%)
  local copies, waits for them, and re-layouts  7.1 us (4%)
    pallas_call x1, Pallas kernels, body(): pl.pallas_call(layer_kernel, out_shape=(jax.ShapeDtypeStruct((rows_blk, w...  181 us
    unnamed x4, local copies, waits for them, and re-layouts  5.72 us

profile of v2, /device:TPU:1, one launch (start us, length us, event | category | flops | bytes accessed | tf_op | source)
XLA Modules:
  0.0 188.9 jit_solution(14246715145468505538)
XLA Ops:
  0.6 1.4 copy.16.coords_ref
  2.0 181.2 %layer.1 = (bf16[512,128]{1,0:T(8,128)(2,1)}, bf16[64,1024]{1,0:T(8,128)(2,1)}, f32[32,128]{1,0:T(8,128)}, f32[3,128]{1,0:T(4,128)}) custom-call(bf16[512,1024]{1,0:T(8,128)(2,1)} %feat_hbm.1, s32[1,512]{1,0:T(1,128)} %bitcast.9, bf16[4,4,256,256]{3,2,1,0:T(8,128)(2,1)} %bitcast.7, s32[4]{0:T(128)} %bitcast.10, s32[4,4,2]{2,1,0:T(4,128)} %copy.16.coords_ref, ...), custom_call_target="tpu_custom_call" | custom-call | tf_op jit(solution)/shard_map/layer/pallas_call | solution.py:565
  183.2 1.6 copy.23
  184.8 1.6 copy.24
  186.3 1.3 copy.25
  187.7 1.3 copy.26

commit v3 on v2

--- a/solution.py
+++ b/solution.py
@@ -61,7 +61,6 @@
         return [(self.b, self.across(d)) for d in range(1, NX)] + [(self.b, self.sib)]
 
 
-DYS = (0, -1, 1, 2)
 ROW_TILE = 128
 COL_TILE = 256
 BY_FIRST = (((0,), (0,)), ((), ()))
@@ -116,8 +115,14 @@
     zr,
     yr,
     yh,
-    piece_recv,
-    half_recv,
+    qin,
+    qside,
+    owed,
+    lent,
+    line_recv,
+    side_recv,
+    plane_send,
+    plane_recv,
     line_send,
     swap_send,
     swap_recv,
@@ -144,6 +149,10 @@
     z_recv,
     y_recv,
     h_recv,
+    chain_send,
+    chain_recv,
+    lent_send,
+    lent_recv,
 ):
     at = Place()
     b, r, nb, nr, nz = at.b, at.r, at.nb, at.nr, at.nz
@@ -157,6 +166,7 @@
     sides = rows_blk // tiles.shape[-1]
     side = tiles.shape[-1]
     slots = tiles.shape[1]
+    steps = nb // nr
 
     loads = [
         pltpu.make_async_copy(src, dst, load_sem.at[i])
@@ -178,34 +188,27 @@
     reordered[x] = reorder(x * ROW_TILE)
     g[b] = reordered[x, pl.ds(pl.multiple_of(k * rows, rows), rows), :]
 
-    def to_line(dyi, dz, dz_step):
-        c = at.block(DYS[dyi], dz)
-        target = (dz - dz_step) % nz
-        remote(
-            g.at[c], g.at[c], line_send, piece_recv.at[dyi, target], at.block(0, dz_step), r
-        ).start()
-
-    def hand_out(dyi, dz):
-        c = at.block(DYS[dyi], dz)
+    opposite = (x + 2) % NX
+    far_blk = nb // steps
+
+    def pass_on(c, sem, blk, low=0, count=rows):
+        part = pl.ds(low, count)
+        return remote(g.at[c, part], g.at[c, part], line_send, sem, blk, r)
+
+    def hand_out(dy, dz):
+        c = at.block(dy, dz)
         diff = (b - c + nb) % nb
         goal = diff % nr
         step = diff // nr
-
-        @pl.when(goal != r)
-        def _():
-            remote(
-                g.at[c], o.at[step, r], swap_send, swap_recv.at[step], b, goal
-            ).start()
+        slot = o.at[step, x, pl.ds(pl.multiple_of(k * rows, rows), rows)]
+
+        @pl.when((goal != r) & (goal // 2 != opposite))
+        def _():
+            remote(g.at[c], slot, swap_send, swap_recv.at[step], b, goal).start()
 
         @pl.when(goal == r)
         def _():
-            pltpu.make_async_copy(g.at[c], o.at[step, r], own_sem.at[step]).start()
-
-    def arrive(dyi, dz):
-        c = at.block(DYS[dyi], dz)
-        remote(
-            g.at[c], g.at[c], line_send, piece_recv.at[dyi, dz % nz], b, r
-        ).wait_recv()
+            pltpu.make_async_copy(g.at[c], slot, own_sem.at[step]).start()
 
     def fill_block(step):
         def run():
@@ -229,7 +232,7 @@
     def fill_rows(d):
         def run():
             n = (x + d) % NX
-            if d:
+            if d % 2:
                 reordered[n] = reorder(n * ROW_TILE)
             if d == 0:
                 loads[2].wait()
@@ -238,51 +241,109 @@
 
         return run
 
-    work = [fill_block(step) for step in range(nb // nr)] + [fill_rows(d) for d in range(NX)]
-
-    for dyi, dy in ((2, -1), (1, 1)):
-        remote(
-            g.at[b], g.at[b], line_send, piece_recv.at[dyi, 0], at.block(dy, 0), r
-        ).start()
-    to_line(0, 0, 1)
-    to_line(0, 0, -1)
-    hand_out(0, 0)
-    for dyi, onward, low in ((1, 1, 0), (2, -1, half)):
-        arrive(dyi, 0)
-        c = at.block(DYS[dyi], 0)
-        part = pl.ds(low, half)
-        remote(
-            g.at[c, part], g.at[c, part], line_send, half_recv.at[dyi - 1], at.block(onward, 0), r
-        ).start()
-        to_line(dyi, 0, 1)
-        to_line(dyi, 0, -1)
-        hand_out(dyi, 0)
-    far = at.block(2, 0)
-    for i, low in ((0, 0), (1, half)):
-        part = pl.ds(low, half)
-        remote(
-            g.at[far, part], g.at[far, part], line_send, half_recv.at[i], b, r
-        ).wait_recv()
-    to_line(3, 0, 1)
-    to_line(3, 0, -1)
-    hand_out(3, 0)
-    for t in range(1, reach):
-        for dyi in range(4):
-            for way in (1, -1):
-                dz = -t * way
-                arrive(dyi, dz)
-                if t < reach - 1 or (way == 1) == (dyi < 2):
-                    to_line(dyi, dz, way)
-                hand_out(dyi, dz)
+    work = [fill_block(step) for step in range(steps)] + [fill_rows(d) for d in range(NX)]
+
+    def slab(step, low=0, count=ROW_TILE):
+        return o.at[step, opposite, pl.ds(low, count)]
+
+    def relay(step_from, step_to, sem, blk, low=0, count=ROW_TILE):
+        return remote(
+            slab(step_from, low, count), slab(step_to, low, count), plane_send.at[0], plane_recv.at[sem], blk, r
+        )
+
+    def shift_out():
+        return remote(
+            reordered.at[opposite], slab(0), plane_send.at[1], plane_recv.at[0], (b + r) % nb, r
+        )
+
+    up, down = (b + far_blk) % nb, (b - far_blk + nb) % nb
+
+    def plane_start():
+        @pl.when(r != 0)
+        def _():
+            shift_out().start()
+
+        @pl.when(r == 0)
+        def _():
+            o[0, opposite] = reordered[opposite]
+
+    def plane_spread():
+        @pl.when(r != 0)
+        def _():
+            shift_out().wait_recv()
+
+        relay(0, 1, 1, up).start()
+        relay(0, 3, 3, down).start()
+
+    def plane_far():
+        relay(0, 1, 1, up).wait_recv()
+        relay(1, 2, 2, up, 0, rows).start()
+        relay(0, 3, 3, down).wait_recv()
+        relay(3, 2, 4, down, rows, rows).start()
+
+    def plane_end():
+        relay(1, 2, 2, up, 0, rows).wait_recv()
+        relay(3, 2, 4, down, rows, rows).wait_recv()
+
+    ORDER = [0] + [dz for t in range(1, reach) for dz in (-t, t)] + [reach]
+
+    def column_step(i):
+        dz = ORDER[i]
+        c = at.block(0, dz)
+        if dz == reach:
+            for w in range(2):
+                pass_on(c, line_recv.at[reach + w], b, w * half, half).wait_recv()
+        elif dz:
+            pass_on(c, line_recv.at[dz % nz + (dz < 0)], b).wait_recv()
+        for w, way in ((0, 1), (1, -1)):
+            if dz == 0 or (dz * way < 0 and abs(dz) < reach - 1):
+                n = (dz - way) % nz
+                pass_on(c, line_recv.at[n + (n > reach)], at.block(0, way)).start()
+            elif dz * way == 1 - reach:
+                pass_on(c, line_recv.at[reach + w], at.block(0, way), w * half, half).start()
+        for w, way in ((0, 1), (1, -1)):
+            pass_on(c, side_recv.at[w, i], at.block(way, 0)).start()
+        hand_out(0, dz)
+
+    def side_step(i):
+        dz = ORDER[i]
+        for w, way in ((0, 1), (1, -1)):
+            c = at.block(-way, dz)
+            pass_on(c, side_recv.at[w, i], b).wait_recv()
+            pass_on(c, side_recv.at[2 + w, i], at.block(way, 0), w * half, half).start()
+            hand_out(-way, dz)
+
+    def far_step(i):
+        dz = ORDER[i]
+        c = at.block(2, dz)
+        for w in range(2):
+            pass_on(c, side_recv.at[2 + w, i], b, w * half, half).wait_recv()
+        hand_out(2, dz)
+
+    lag = 3
+    for i in range(nz + lag + 1):
+        if i < nz:
+            column_step(i)
+        if i == 0:
+            reordered[opposite] = reorder(opposite * ROW_TILE)
+            plane_start()
+        if lag <= i < nz + lag:
+            side_step(i - lag)
+        if lag < i:
+            far_step(i - lag - 1)
+        if i == 3:
+            plane_spread()
+        if i == 7:
+            plane_far()
+        if i >= 2:
             if work:
                 work.pop(0)()
-    for dyi in (0, 2, 1, 3):
-        arrive(dyi, reach)
-        hand_out(dyi, reach)
+    plane_end()
 
     for i, step in enumerate((0, 1, 3, 2)):
-        pltpu.make_async_copy(o.at[step, 0], o.at[step, 0], own_sem.at[step]).wait()
-        some = o.at[step, pl.ds(0, nr - 1)]
+        some = o.at[step, 0, pl.ds(0, rows)]
+        pltpu.make_async_copy(some, some, own_sem.at[step]).wait()
+        some = g.at[pl.ds(0, nr - 3)]
         remote(some, some, swap_send, swap_recv.at[step], b, r).wait_recv()
 
         def part_tile(n, carry, step=step, i=i):
@@ -412,6 +473,25 @@
 
     lax.fori_loop(0, wide // COL_TILE, agg_tile, 0)
 
+    def owed_slab(step, low=0, count=ROW_TILE):
+        return cb.at[step, opposite, pl.ds(low, count)]
+
+    def chain_half(w, blk):
+        return remote(
+            owed_slab(2, w * rows, rows), qside.at[w], chain_send.at[0], chain_recv.at[w], blk, r
+        )
+
+    def chain_whole(w, blk):
+        return remote(
+            owed_slab((1, 3)[w]), qin.at[w], chain_send.at[0], chain_recv.at[2 + w], blk, r
+        )
+
+    def chain_shift():
+        return remote(
+            owed_slab(0), owed, chain_send.at[1], chain_recv.at[4], (b - r + nb) % nb, r
+        )
+
+    near = [sib] + [((x + d) % NX) * 2 + j for d in (1, 3) for j in range(2)]
     for step in (2, 1, 3, 0):
 
         def back_tile(n, carry, step=step):
@@ -419,17 +499,23 @@
             out = lax.dot_general(
                 adj[step], grad_agg[:, cols], BY_FIRST, preferred_element_type=F32
             )
-            cb[step, :, :, cols] = out.astype(BF16).reshape(nr, rows, COL_TILE)
+            cb[step, :, :, cols] = out.astype(BF16).reshape(NX, ROW_TILE, COL_TILE)
             return carry
 
         lax.fori_loop(0, wide // COL_TILE, back_tile, 0)
         c = (b - r - nr * step + 2 * nb) % nb
-        pltpu.make_async_copy(cb.at[step, r], pbuf.at[c], back_own.at[step]).start()
-        for d in (1, 7, 2, 6, 3, 5, 4):
-            goal = (r + d) % nr
+        for goal in near:
+            low = pl.multiple_of(goal % 2 * rows, rows)
             remote(
-                cb.at[step, goal], pbuf.at[c], back_send, part_recv.at[c], b, goal
+                cb.at[step, goal // 2, pl.ds(low, rows)], pbuf.at[c], back_send, part_recv.at[c], b, goal
             ).start()
+        low = pl.multiple_of(k * rows, rows)
+        pltpu.make_async_copy(
+            cb.at[step, x, pl.ds(low, rows)], pbuf.at[c], back_own.at[step]
+        ).start()
+        if step == 2:
+            chain_half(0, down).start()
+            chain_half(1, up).start()
     for d in range(4):
         came = (1 - k) * NX + (x - d + NX) % NX
         remote(agg.at[came], agg.at[came], agg_send.at[3], agg_sib.at[d], b, sib).wait_recv()
@@ -448,68 +534,130 @@
     self_rows[...] = lax.dot_general(
         grad_all[own_rows, :], w_self[...], BY_LAST, preferred_element_type=F32
     )
-    for step in range(4):
+    for w, blk in ((0, down), (1, up)):
+        step = (1, 3)[w]
+        part = pl.ds(w * rows, rows)
+        chain_half(w, blk).wait_recv()
+        cb[step, opposite, part] = (
+            cb[step, opposite, part].astype(F32) + qside[w].astype(F32)
+        ).astype(BF16)
+        chain_whole(w, blk).start()
+    for step in range(steps):
         c = (b - r - nr * step + 2 * nb) % nb
-        pltpu.make_async_copy(cb.at[step, r], pbuf.at[c], back_own.at[step]).wait()
-
-    def own(dyi, dz):
-        c = at.block(DYS[dyi], dz)
-
-        @pl.when((b - c + nb) % nr != r)
+        pltpu.make_async_copy(pbuf.at[c], pbuf.at[c], back_own.at[step]).wait()
+
+    def chain_sum():
+        for w, blk in ((0, down), (1, up)):
+            chain_whole(w, blk).wait_recv()
+        cb[0, opposite] = (
+            cb[0, opposite].astype(F32) + qin[0].astype(F32) + qin[1].astype(F32)
+        ).astype(BF16)
+
+        @pl.when(r != 0)
+        def _():
+            chain_shift().start()
+
+        @pl.when(r == 0)
+        def _():
+            owed[...] = cb[0, opposite]
+
+    def lend(j):
+        return remote(
+            owed.at[pl.ds(j * rows, rows)], lent.at[k], lent_send, lent_recv.at[k], b, opposite * 2 + j
+        )
+
+    def chain_lend():
+        @pl.when(r != 0)
+        def _():
+            chain_shift().wait_recv()
+
+        for j in range(2):
+            lend(j).start()
+
+    def own(dy, dz):
+        c = at.block(dy, dz)
+        source = (b - c + nb) % nr
+
+        @pl.when((source != r) & (source // 2 != opposite))
         def _():
             remote(pbuf.at[c], pbuf.at[c], back_send, part_recv.at[c], b, r).wait_recv()
 
+        @pl.when(source // 2 == opposite)
+        def _():
+            pbuf[c] = jnp.zeros((rows, wide), BF16)
+
         return c
 
-    for t in range(reach, 0, -1):
-        for dyi in range(4):
-            for wi, way in ((0, 1), (1, -1)):
-                first = reach if (way == 1) == (dyi < 2) else reach - 1
-                if t > first:
-                    continue
-                c = own(dyi, t * way)
-                if t < first:
-                    remote(
-                        pbuf.at[c], zr.at[wi, dyi, t], back_line, z_recv.at[wi, dyi, t], b, r
-                    ).wait_recv()
-                    pbuf[c] = (pbuf[c].astype(F32) + zr[wi, dyi, t].astype(F32)).astype(BF16)
-                remote(
-                    pbuf.at[c],
-                    zr.at[wi, dyi, t - 1],
-                    back_line,
-                    z_recv.at[wi, dyi, t - 1],
-                    at.block(0, way),
-                    r,
-                ).start()
-
-    def column(dyi):
-        c = own(dyi, 0)
-        for wi in range(2):
+    BACK = [reach] + [dz for t in range(reach - 1, 0, -1) for dz in (t, -t)] + [0]
+
+    def back_far(i):
+        c = own(2, BACK[i])
+        for w, way in ((0, 1), (1, -1)):
+            part = pl.ds(w * half, half)
             remote(
-                pbuf.at[c], zr.at[wi, dyi, 0], back_line, z_recv.at[wi, dyi, 0], b, r
-            ).wait_recv()
-        return c, pbuf[c].astype(F32) + zr[0, dyi, 0].astype(F32) + zr[1, dyi, 0].astype(F32)
-
-    c, value = column(3)
-    pbuf[c] = value.astype(BF16)
-    for i, dy in ((0, 1), (1, -1)):
-        part = pl.ds(i * half, half)
-        remote(
-            pbuf.at[c, part], yh.at[i], back_line, h_recv.at[i], at.block(dy, 0), r
-        ).start()
-    for i, (dyi, dy) in enumerate(((2, 1), (1, -1))):
-        c, value = column(dyi)
-        pbuf[c] = value.astype(BF16)
-        remote(yh.at[i], yh.at[i], back_line, h_recv.at[i], b, r).wait_recv()
-        part = pl.ds(i * half, half)
-        pbuf[c, part] = (value[i * half : (i + 1) * half] + yh[i].astype(F32)).astype(BF16)
-        remote(pbuf.at[c], yr.at[i], back_line, y_recv.at[i], at.block(dy, 0), r).start()
-    c, value = column(0)
-    value = value + self_rows[...]
-    for i in range(2):
-        remote(yr.at[i], yr.at[i], back_line, y_recv.at[i], b, r).wait_recv()
-        value = value + yr[i].astype(F32)
-    out_ref[...] = value.astype(BF16)
+                pbuf.at[c, part], yh.at[w, i], back_line, h_recv.at[w, i], at.block(way, 0), r
+            ).start()
+
+    def back_side(i):
+        for w, way in ((0, 1), (1, -1)):
+            c = own(way, BACK[i])
+            remote(yh.at[w, i], yh.at[w, i], back_line, h_recv.at[w, i], b, r).wait_recv()
+            part = pl.ds(w * half, half)
+            pbuf[c, part] = (pbuf[c, part].astype(F32) + yh[w, i].astype(F32)).astype(BF16)
+            remote(
+                pbuf.at[c], yr.at[w, i], back_line, y_recv.at[w, i], at.block(way, 0), r
+            ).start()
+
+    def z_send(c, w, t, low=0, count=rows):
+        part = pl.ds(low, count)
+        return remote(
+            pbuf.at[c, part], zr.at[w, t, part], back_line, z_recv.at[w, t], at.block(0, (1, -1)[w]), r
+        )
+
+    def back_column(i):
+        dz = BACK[i]
+        c = own(0, dz)
+        for w in range(2):
+            remote(yr.at[w, i], yr.at[w, i], back_line, y_recv.at[w, i], b, r).wait_recv()
+        value = pbuf[c].astype(F32) + yr[0, i].astype(F32) + yr[1, i].astype(F32)
+        if dz == reach:
+            pbuf[c] = value.astype(BF16)
+            for w in range(2):
+                z_send(c, w, reach - 1, w * half, half).start()
+            return None
+        if dz == 0:
+            for w in range(2):
+                z_send(c, w, 0).wait_recv()
+                value = value + zr[w, 0].astype(F32)
+            return value
+        w, t = (0, dz) if dz > 0 else (1, -dz)
+        if t == reach - 1:
+            low = w * half
+            z_send(c, w, t, low, half).wait_recv()
+            pbuf[c] = value.astype(BF16)
+            part = pl.ds(low, half)
+            pbuf[c, part] = (value[low : low + half] + zr[w, t, part].astype(F32)).astype(BF16)
+        else:
+            z_send(c, w, t).wait_recv()
+            pbuf[c] = (value + zr[w, t].astype(F32)).astype(BF16)
+        z_send(c, w, t - 1).start()
+        return None
+
+    for i in range(nz + 2):
+        if i < nz:
+            back_far(i)
+        if 1 <= i < nz + 1:
+            back_side(i - 1)
+        if i >= 2:
+            value = back_column(i - 2)
+        if i == 3:
+            chain_sum()
+        if i == 6:
+            chain_lend()
+    for j in range(2):
+        remote(lent.at[j], lent.at[j], lent_send, lent_recv.at[j], b, r).wait_recv()
+        value = value + lent[j].astype(F32)
+    out_ref[...] = (value + self_rows[...]).astype(BF16)
 
     some = term_in.at[pl.ds(0, nb - 1)]
     remote(some, some, term_send, term_recv, b, sib).wait()
@@ -519,9 +667,18 @@
         remote(some, some, sem, term_recv, b, sib).wait_send()
 
     sent(g.at[pl.ds(0, 3 + 4 * (nz - 1))], line_send)
-    sent(g.at[pl.ds(0, 4 * (nr - 1))], swap_send)
+    sent(g.at[pl.ds(0, steps * (nr - 3))], swap_send)
+    sent(o.at[0, pl.ds(0, NX - 1)], plane_send.at[0])
+    sent(cb.at[0, pl.ds(0, NX - 1)], chain_send.at[0])
+
+    @pl.when(r != 0)
+    def _():
+        shift_out().wait_send()
+        chain_shift().wait_send()
+
+    sent(lent, lent_send)
     sent(pbuf.at[pl.ds(0, 3 + 4 * (nz - 1))], back_line)
-    sent(pbuf.at[pl.ds(0, 4 * (nr - 1))], back_send)
+    sent(pbuf.at[pl.ds(0, steps * (nr - 3))], back_send)
     sent(pb, red_send.at[0])
     for d in range(1, NX):
         sent(qb.at[d - 1], red_send.at[d])
@@ -551,7 +708,8 @@
     rows = rows_blk // nr
     thin = wide // nb
     steps = nb // nr
-    reach = nb // NY // 2
+    nz = nb // NY
+    reach = nz // 2
     tiles = adj_tiles[0, 0]
     dma = pltpu.SemaphoreType.DMA
     vmem = pl.BlockSpec(memory_space=pltpu.VMEM)
@@ -582,7 +740,7 @@
                 room(steps, rows_blk, rows_blk),
                 room(NX, ROW_TILE, width, dtype=F32),
                 room(nb, rows, wide),
-                room(steps, nr, rows, wide),
+                room(steps, NX, ROW_TILE, wide),
                 room(rows_blk, wide, dtype=F32),
                 room(NX, rows, wide),
                 room(NX, rows, wide),
@@ -600,13 +758,19 @@
                 room(rows, wide, dtype=F32),
                 room(nb, thin, width),
                 room(nb, thin, width),
-                room(steps, nr, rows, wide),
+                room(steps, NX, ROW_TILE, wide),
                 room(nb, rows, wide),
-                room(2, 4, reach, rows, wide),
+                room(2, reach, rows, wide),
+                room(2, nz, rows, wide),
+                room(2, nz, rows // 2, wide),
+                room(2, ROW_TILE, wide),
                 room(2, rows, wide),
-                room(2, rows // 2, wide),
-                dma((4, nb // NY)),
+                room(ROW_TILE, wide),
+                room(2, rows, wide),
+                dma((nz + 1,)),
+                dma((4, nz)),
                 dma((2,)),
+                dma((5,)),
                 dma(()),
                 dma(()),
                 dma((steps,)),
@@ -630,8 +794,12 @@
                 dma(()),
                 dma((nb,)),
                 dma(()),
-                dma((2, 4, reach)),
+                dma((2, reach)),
+                dma((2, nz)),
+                dma((2, nz)),
                 dma((2,)),
+                dma((5,)),
+                dma(()),
                 dma((2,)),
             ],
             compiler_params=pltpu.CompilerParams(

time: 189 us -> 164 us (0.87)
  Pallas kernels: 181 us -> 156 us
    pallas_call x1, Pallas kernels: 181 us -> 156 us  [body(): pl.pallas_call(layer_kernel, out_shape=(jax.ShapeDtypeStruct((rows_blk, w...]
where the time goes in v3:
time: 164 us; the launch traced here: 163 us
  Pallas kernels  156 us (95%)
  local copies, waits for them, and re-layouts  7.1 us (4%)
    pallas_call x1, Pallas kernels, body(): pl.pallas_call(layer_kernel, out_shape=(jax.ShapeDtypeStruct((rows_blk, w...  156 us
    unnamed x4, local copies, waits for them, and re-layouts  5.72 us

profile of v3, /device:TPU:1, one launch (start us, length us, event | category | flops | bytes accessed | tf_op | source)
XLA Modules:
  0.0 163.3 jit_solution(16069805834173553318)
XLA Ops:
  0.6 1.4 copy.16.coords_ref
  2.0 155.6 %layer.1 = (bf16[512,128]{1,0:T(8,128)(2,1)}, bf16[64,1024]{1,0:T(8,128)(2,1)}, f32[32,128]{1,0:T(8,128)}, f32[3,128]{1,0:T(4,128)}) custom-call(bf16[512,1024]{1,0:T(8,128)(2,1)} %feat_hbm.1, s32[1,512]{1,0:T(1,128)} %bitcast.9, bf16[4,4,256,256]{3,2,1,0:T(8,128)(2,1)} %bitcast.7, s32[4]{0:T(128)} %bitcast.10, s32[4,4,2]{2,1,0:T(4,128)} %copy.16.coords_ref, ...), custom_call_target="tpu_custom_call" | custom-call | tf_op jit(solution)/shard_map/layer/pallas_call | solution.py:723
  157.6 1.6 copy.23
  159.2 1.6 copy.24
  160.7 1.3 copy.25
  162.1 1.3 copy.26

commit v4 on v3

--- a/solution.py
+++ b/solution.py
@@ -28,7 +28,10 @@
     barrier = pltpu.get_barrier_semaphore()
     for blk, rep in peers:
         pl.semaphore_signal(barrier, inc=1, device_id=(blk, rep), device_id_type=MESH)
-    pl.semaphore_wait(barrier, len(peers))
+
+
+def greeted(count):
+    pl.semaphore_wait(pltpu.get_barrier_semaphore(), count)
 
 
 class Place:
@@ -50,15 +53,8 @@
     def across(self, dx):
         return ((self.x + dx) % NX) * 2 + self.k
 
-    def torus_peers(self):
-        steps = ((1, 0), (-1, 0), (0, 1), (0, -1))
-        return [(self.block(dy, dz), self.r) for dy, dz in steps]
-
     def rep_peers(self):
         return [(self.b, (self.r + d) % self.nr) for d in range(1, self.nr)]
-
-    def line_peers(self):
-        return [(self.b, self.across(d)) for d in range(1, NX)] + [(self.b, self.sib)]
 
 
 ROW_TILE = 128
@@ -98,11 +94,14 @@
     rb1,
     qb,
     rb2,
+    rb3,
     agg,
     prod,
     prod_in,
     pre,
     stat,
+    stats_y,
+    line_stat,
     stats,
     grad_pre,
     grad_all,
@@ -110,6 +109,8 @@
     self_rows,
     term,
     term_in,
+    term_mid,
+    term_last,
     cb,
     pbuf,
     zr,
@@ -134,12 +135,10 @@
     prod_recv,
     agg_send,
     agg_recv,
-    agg_sib,
     stat_send,
     stat_recv,
     col_send,
     col_recv,
-    col_sib,
     term_send,
     term_recv,
     back_own,
@@ -183,11 +182,12 @@
         pick = jnp.where(ids == want, 1.0, 0.0).astype(BF16)
         return lax.dot_general(pick, feat[...], BY_FIRST, preferred_element_type=F32).astype(BF16)
 
-    greet([((b + d) % nb, r) for d in range(1, nb)] + at.rep_peers())
+    peers = [((b + d) % nb, r) for d in range(1, nb)] + at.rep_peers()
+    greet(peers)
     loads[0].wait()
     reordered[x] = reorder(x * ROW_TILE)
     g[b] = reordered[x, pl.ds(pl.multiple_of(k * rows, rows), rows), :]
-
+    greeted(len(peers))
     opposite = (x + 2) % NX
     far_blk = nb // steps
 
@@ -320,7 +320,7 @@
             pass_on(c, side_recv.at[2 + w, i], b, w * half, half).wait_recv()
         hand_out(2, dz)
 
-    lag = 3
+    lag = 2
     for i in range(nz + lag + 1):
         if i < nz:
             column_step(i)
@@ -331,9 +331,9 @@
             side_step(i - lag)
         if lag < i:
             far_step(i - lag - 1)
-        if i == 3:
+        if i == 4:
             plane_spread()
-        if i == 7:
+        if i == 8:
             plane_far()
         if i >= 2:
             if work:
@@ -358,51 +358,107 @@
     def chunk(m):
         return acc[pl.ds(pl.multiple_of(m * rows, rows), rows), :]
 
-    for m in range(NX):
+    def to_sibling(m):
+        return remote(pb.at[m], rb1.at[m], red_send.at[0], red_recv1.at[m], b, sib)
+
+    def both(m):
+        return chunk(k * NX + m) + rb1[m].astype(F32)
+
+    turns = [(x + d) % NX for d in (2, 1, 3, 0)]
+    for m in turns:
         pb[m] = chunk((1 - k) * NX + m).astype(BF16)
-    swap_halves = remote(pb, rb1, red_send.at[0], red_recv1, b, sib)
-    swap_halves.start()
+        to_sibling(m).start()
     loads[3].wait()
-    swap_halves.wait_recv()
-
-    def reduced(d):
+
+    def half_way(w):
+        part = pl.ds(w * half, half)
         return remote(
-            qb.at[d - 1], rb2.at[d - 1], red_send.at[d], red_recv2.at[d - 1], b, at.across(d)
-        )
-
-    for d in (2, 1, 3):
-        goal = (x + d) % NX
-        qb[d - 1] = (chunk(k * NX + goal) + rb1[goal].astype(F32)).astype(BF16)
-        reduced(d).start()
+            qb.at[0, part], rb3.at[w], red_send.at[1], red_recv2.at[w], b, at.across((1, 3)[w])
+        )
+
+    def one_way(w):
+        return remote(
+            qb.at[1 + w], rb2.at[w], red_send.at[1], red_recv2.at[2 + w], b, at.across((1, 3)[w])
+        )
+
+    to_sibling(turns[0]).wait_recv()
+    qb[0] = both(turns[0]).astype(BF16)
+    for w in range(2):
+        half_way(w).start()
+    for w in range(2):
+        to_sibling(turns[1 + w]).wait_recv()
+        value = both(turns[1 + w])
+        qb[1 + w] = value.astype(BF16)
+        half_way(w).wait_recv()
+        part = pl.ds(w * half, half)
+        qb[1 + w, part] = (value[w * half : (w + 1) * half] + rb3[w].astype(F32)).astype(BF16)
+        one_way(w).start()
     home = k * NX + x
-    total = chunk(home) + rb1[x].astype(F32)
-    for d in (1, 3, 2):
-        reduced(d).wait_recv()
-        total = total + rb2[d - 1].astype(F32)
+    to_sibling(x).wait_recv()
+    total = both(x)
+    for w in range(2):
+        one_way(w).wait_recv()
+        total = total + rb2[w].astype(F32)
     agg[home] = total.astype(BF16)
 
     for n in range(wide // COL_TILE):
         cols = slice(n * COL_TILE, (n + 1) * COL_TILE)
         out = jnp.dot(agg[home], w_neigh[:, cols], preferred_element_type=F32)
         for j in range(COL_TILE // width):
-            prod[n * (COL_TILE // width) + j] = out[:, j * width : (j + 1) * width]
+            prod[n * (COL_TILE // width) + j] = out[:, j * width : (j + 1) * width].astype(BF16)
     for d in (4, 5, 2, 3, 6, 7, 1):
         goal = (r + d) % nr
         remote(prod.at[goal], prod_in.at[home], prod_send, prod_recv, b, goal).start()
     prod_in[home] = prod[r]
 
-    def agg_line(d):
-        return remote(
-            agg.at[home], agg.at[home], agg_send.at[d - 1], agg_recv.at[d - 1], b, at.across(d)
-        )
-
-    for d in (2, 1, 3):
-        agg_line(d).start()
-    remote(agg.at[home], agg.at[home], agg_send.at[3], agg_sib.at[0], b, sib).start()
+    class Line:
+        def __init__(self, ref, tall, send, recv):
+            self.ref, self.tall, self.send, self.recv = ref, tall, send, recv
+
+        def move(self, chip, core, sem, goal, low=0, count=None):
+            ref = self.ref(chip, core, low, self.tall if count is None else count)
+            return remote(ref, ref, self.send, self.recv.at[sem], b, goal)
+
+        def begin(self):
+            self.move(x, k, 4, sib).start()
+            self.move(x, k, 0, at.across(1)).start()
+            self.move(x, k, 1, at.across(3)).start()
+
+        def middle(self):
+            side = self.tall // 2
+            for w, d in ((0, 3), (1, 1)):
+                chip = (x + d) % NX
+                self.move(chip, k, w, sib).wait_recv()
+                self.move(chip, k, 2 + w, at.across(4 - d), w * side, side).start()
+                self.move(chip, k, 5 + w, sib).start()
+
+        def end(self):
+            side = self.tall // 2
+            chip = (x + 2) % NX
+            for w in range(2):
+                self.move(chip, k, 2 + w, sib, w * side, side).wait_recv()
+            self.move(chip, k, 7, sib).start()
+
+        def wait(self):
+            for i, d in enumerate((0, 3, 1, 2)):
+                self.move((x + d) % NX, 1 - k, 4 + i, sib).wait_recv()
+
+    def agg_chunk(chip, core, low, count):
+        return agg.at[core * NX + chip, pl.ds(low, count)]
+
+    def grad_chunk(chip, core, low, count):
+        cols = pl.ds(pl.multiple_of((chip * 2 + core) * width, width), width)
+        return grad_all.at[pl.ds(low, count), cols]
+
+    agg_line = Line(agg_chunk, rows, agg_send, agg_recv)
+    grad_line = Line(grad_chunk, rows_blk, col_send, col_recv)
+    agg_line.begin()
     some = prod_in.at[pl.ds(0, nr - 1)]
     remote(some, some, prod_send, prod_recv, b, sib).wait_recv()
 
-    pre[...] = self_pre[...].reshape(rows_blk, width) + prod_in[...].reshape(rows_blk, width)
+    pre[...] = self_pre[...].reshape(rows_blk, width) + prod_in[...].astype(F32).reshape(
+        rows_blk, width
+    )
     upstream = cot_ref[...].astype(F32)
     near_mean = jnp.sum(pre[...], axis=0, keepdims=True) / rows_blk
     off = pre[...] - near_mean
@@ -411,18 +467,37 @@
     stat[2:3, :] = jnp.sum(upstream, axis=0, keepdims=True)
     stat[3:4, :] = jnp.sum(upstream * off, axis=0, keepdims=True)
     stat[4:8, :] = jnp.zeros((4, width), F32)
-    for d in range(1, nb):
-        remote(stat, stats.at[b], stat_send, stat_recv, (b + d) % nb, r).start()
-    stats[b] = stat[...]
-    some = stats.at[pl.ds(0, nb - 1)]
-    remote(some, some, stat_send, stat_recv, b, sib).wait_recv()
+    stats_y[at.y] = stat[...]
+    for d in (2, 1, 3):
+        remote(
+            stat, stats_y.at[at.y], stat_send.at[0], stat_recv.at[0], at.block(d, 0), r
+        ).start()
+    some = stats_y.at[pl.ds(0, NY - 1)]
+    remote(some, some, stat_send.at[0], stat_recv.at[0], b, sib).wait_recv()
+    line_means, line_cots = stats_y[:, 0, :], stats_y[:, 2, :]
+    line_mean = jnp.sum(line_means, axis=0, keepdims=True) / NY
+    apart = line_means - line_mean
+    line_stat[0:1, :] = line_mean
+    line_stat[1:2, :] = jnp.sum(
+        stats_y[:, 1, :] + rows_blk * apart * apart, axis=0, keepdims=True
+    )
+    line_stat[2:3, :] = jnp.sum(line_cots, axis=0, keepdims=True)
+    line_stat[3:4, :] = jnp.sum(stats_y[:, 3, :] + line_cots * apart, axis=0, keepdims=True)
+    line_stat[4:8, :] = jnp.zeros((4, width), F32)
+    stats[at.z] = line_stat[...]
+    for d in (4, 3, 5, 2, 6, 1, 7):
+        remote(
+            line_stat, stats.at[at.z], stat_send.at[1], stat_recv.at[1], at.block(0, d), r
+        ).start()
+    some = stats.at[pl.ds(0, nz - 1)]
+    remote(some, some, stat_send.at[1], stat_recv.at[1], b, sib).wait_recv()
 
     gain, mean_scale = gain_ref[...], scale_ref[...]
     means, cots = stats[:, 0, :], stats[:, 2, :]
-    col_mean = jnp.sum(means, axis=0, keepdims=True) / nb
+    col_mean = jnp.sum(means, axis=0, keepdims=True) / nz
     moved = means - mean_scale * col_mean
     spread = (
-        jnp.sum(stats[:, 1, :] + rows_blk * moved * moved, axis=0, keepdims=True) / nodes
+        jnp.sum(stats[:, 1, :] + NY * rows_blk * moved * moved, axis=0, keepdims=True) / nodes
     )
     cot_sum = jnp.sum(cots, axis=0, keepdims=True)
     cot_cent = jnp.sum(stats[:, 3, :] + cots * moved, axis=0, keepdims=True)
@@ -436,32 +511,17 @@
         sharp * upstream - centered * weight - mean_scale * grad_cent_total / nodes
     ).astype(BF16)
 
-    def columns(rep):
-        return grad_all.at[:, pl.ds(pl.multiple_of(rep * width, width), width)]
-
-    for d in (2, 1, 3):
-        remote(
-            grad_pre, columns(r), col_send.at[d - 1], col_recv.at[d - 1], b, at.across(d)
-        ).start()
-    remote(grad_pre, columns(r), col_send.at[3], col_sib.at[0], b, sib).start()
     grad_all[:, pl.ds(pl.multiple_of(r * width, width), width)] = grad_pre[...]
+    grad_line.begin()
     normed_ref[...] = (sharp * centered + bias_ref[...]).astype(BF16)
     norm_ref[0:1, :] = cot_cent / col_scale / nodes
     norm_ref[1:2, :] = cot_sum / nodes
     norm_ref[2:3, :] = -col_mean * grad_cent_total / nodes
-    for d in (1, 3, 2):
-        came = k * NX + (x - d + NX) % NX
-        remote(
-            agg.at[came], agg.at[came], agg_send.at[d - 1], agg_recv.at[d - 1], b, sib
-        ).wait_recv()
-        remote(agg.at[came], agg.at[came], agg_send.at[3 + d], agg_sib.at[d], b, sib).start()
-    for d in (1, 3, 2):
-        came = columns(at.across(NX - d))
-        remote(came, came, col_send.at[d - 1], col_recv.at[d - 1], b, sib).wait_recv()
-        remote(came, came, col_send.at[3 + d], col_sib.at[d], b, sib).start()
-    for d in range(4):
-        came = columns(((x - d + NX) % NX) * 2 + (1 - k))
-        remote(came, came, col_send.at[3], col_sib.at[d], b, sib).wait_recv()
+    agg_line.middle()
+    grad_line.middle()
+    agg_line.end()
+    grad_line.end()
+    grad_line.wait()
 
     def agg_tile(n, carry):
         low = pl.ds(pl.multiple_of(n * COL_TILE, COL_TILE), COL_TILE)
@@ -472,6 +532,35 @@
         return carry
 
     lax.fori_loop(0, wide // COL_TILE, agg_tile, 0)
+
+    def term_y():
+        agg_line.wait()
+        thin = weight_ref.shape[0]
+        for n in range(wide // COL_TILE):
+            cols = slice(n * COL_TILE, (n + 1) * COL_TILE)
+            source = agg[:, :, cols].reshape(rows_blk, COL_TILE)
+            out = lax.dot_general(source, grad_pre[...], BY_FIRST, preferred_element_type=F32)
+            each = COL_TILE // thin
+            for j in range(each):
+                at_z, at_y = divmod(n * each + j, NY)
+                term[at_y, at_z] = out[j * thin : (j + 1) * thin].astype(BF16)
+        for d in (2, 1, 3):
+            goal = (at.y + d) % NY
+            remote(
+                term.at[goal], term_in.at[at.y], term_send.at[0], term_recv.at[0], at.block(d, 0), r
+            ).start()
+        term_in[at.y] = term[at.y]
+
+    def term_z():
+        some = term_in.at[pl.ds(0, NY - 1)]
+        remote(some, some, term_send.at[0], term_recv.at[0], b, sib).wait_recv()
+        term_mid[...] = jnp.sum(term_in[...].astype(F32), axis=0).astype(BF16)
+        for d in (4, 3, 5, 2, 6, 1, 7):
+            goal = (at.z + d) % nz
+            remote(
+                term_mid.at[goal], term_last.at[at.z], term_send.at[1], term_recv.at[1], at.block(0, d), r
+            ).start()
+        term_last[at.z] = term_mid[at.z]
 
     def owed_slab(step, low=0, count=ROW_TILE):
         return cb.at[step, opposite, pl.ds(low, count)]
@@ -516,20 +605,7 @@
         if step == 2:
             chain_half(0, down).start()
             chain_half(1, up).start()
-    for d in range(4):
-        came = (1 - k) * NX + (x - d + NX) % NX
-        remote(agg.at[came], agg.at[came], agg_send.at[3], agg_sib.at[d], b, sib).wait_recv()
-    thin = weight_ref.shape[0]
-    for n in range(wide // COL_TILE):
-        cols = slice(n * COL_TILE, (n + 1) * COL_TILE)
-        source = agg[:, :, cols].reshape(rows_blk, COL_TILE)
-        out = lax.dot_general(source, grad_pre[...], BY_FIRST, preferred_element_type=F32)
-        each = COL_TILE // thin
-        term[n * each : (n + 1) * each] = out.astype(BF16).reshape(each, thin, width)
-    for d in range(1, nb):
-        goal = (b + d) % nb
-        remote(term.at[goal], term_in.at[b], term_send, term_recv, goal, r).start()
-    term_in[b] = term[b]
+    term_y()
     own_rows = pl.ds(pl.multiple_of(r * rows, rows), rows)
     self_rows[...] = lax.dot_general(
         grad_all[own_rows, :], w_self[...], BY_LAST, preferred_element_type=F32
@@ -643,28 +719,30 @@
         z_send(c, w, t - 1).start()
         return None
 
-    for i in range(nz + 2):
+    for i in range(nz + 4):
         if i < nz:
             back_far(i)
-        if 1 <= i < nz + 1:
-            back_side(i - 1)
-        if i >= 2:
-            value = back_column(i - 2)
-        if i == 3:
+        if 2 <= i < nz + 2:
+            back_side(i - 2)
+        if i >= 4:
+            value = back_column(i - 4)
+        if i == 4:
             chain_sum()
-        if i == 6:
+        if i == 5:
+            term_z()
+        if i == 7:
             chain_lend()
     for j in range(2):
         remote(lent.at[j], lent.at[j], lent_send, lent_recv.at[j], b, r).wait_recv()
         value = value + lent[j].astype(F32)
     out_ref[...] = (value + self_rows[...]).astype(BF16)
 
-    some = term_in.at[pl.ds(0, nb - 1)]
-    remote(some, some, term_send, term_recv, b, sib).wait()
-    weight_ref[...] = jnp.sum(term_in[...].astype(F32), axis=0) / nodes
+    some = term_last.at[pl.ds(0, nz - 1)]
+    remote(some, some, term_send.at[1], term_recv.at[1], b, sib).wait_recv()
+    weight_ref[...] = jnp.sum(term_last[...].astype(F32), axis=0) / nodes
 
     def sent(some, sem):
-        remote(some, some, sem, term_recv, b, sib).wait_send()
+        remote(some, some, sem, term_recv.at[0], b, sib).wait_send()
 
     sent(g.at[pl.ds(0, 3 + 4 * (nz - 1))], line_send)
     sent(g.at[pl.ds(0, steps * (nr - 3))], swap_send)
@@ -680,13 +758,20 @@
     sent(pbuf.at[pl.ds(0, 3 + 4 * (nz - 1))], back_line)
     sent(pbuf.at[pl.ds(0, steps * (nr - 3))], back_send)
     sent(pb, red_send.at[0])
-    for d in range(1, NX):
-        sent(qb.at[d - 1], red_send.at[d])
-    for i in range(7):
-        sent(agg.at[0], agg_send.at[i])
-        sent(grad_pre, col_send.at[i])
+    sent(qb, red_send.at[1])
+    sent(agg.at[pl.ds(0, 7)], agg_send)
+    sent(grad_all.at[:, pl.ds(0, 7 * width)], col_send)
     sent(prod_in.at[pl.ds(0, nr - 1)], prod_send)
-    sent(stats.at[pl.ds(0, nb - 1)], stat_send)
+    sent(stats_y.at[pl.ds(0, NY - 1)], stat_send.at[0])
+    sent(stats.at[pl.ds(0, nz - 1)], stat_send.at[1])
+    sent(term_in.at[pl.ds(0, NY - 1)], term_send.at[0])
+    sent(term_last.at[pl.ds(0, nz - 1)], term_send.at[1])
+
+
+def write_kernel(*refs):
+    n = len(refs) // 2
+    for i in range(n):
+        refs[n + i][...] = refs[i][...]
 
 
 def body(
@@ -719,7 +804,7 @@
     def room(*shape, dtype=BF16):
         return pltpu.VMEM(shape, dtype)
 
-    return tuple(
+    outs = tuple(
         pl.pallas_call(
             layer_kernel,
             out_shape=(
@@ -745,19 +830,24 @@
                 room(NX, rows, wide),
                 room(NX, rows, wide),
                 room(NX - 1, rows, wide),
-                room(NX - 1, rows, wide),
+                room(2, rows, wide),
+                room(2, rows // 2, wide),
                 room(nr, rows, wide),
-                room(nr, rows, width, dtype=F32),
-                room(nr, rows, width, dtype=F32),
+                room(nr, rows, width),
+                room(nr, rows, width),
                 room(rows_blk, width, dtype=F32),
                 room(8, width, dtype=F32),
-                room(nb, 8, width, dtype=F32),
+                room(NY, 8, width, dtype=F32),
+                room(8, width, dtype=F32),
+                room(nz, 8, width, dtype=F32),
                 room(rows_blk, width),
                 room(rows_blk, wide),
                 room(rows_blk, wide),
                 room(rows, wide, dtype=F32),
-                room(nb, thin, width),
-                room(nb, thin, width),
+                room(NY, nz, thin, width),
+                room(NY, nz, thin, width),
+                room(nz, thin, width),
+                room(nz, thin, width),
                 room(steps, NX, ROW_TILE, wide),
                 room(nb, rows, wide),
                 room(2, reach, rows, wide),
@@ -775,21 +865,19 @@
                 dma(()),
                 dma((steps,)),
                 dma((steps,)),
+                dma((2,)),
                 dma((4,)),
-                dma(()),
-                dma((3,)),
-                dma(()),
-                dma(()),
-                dma((7,)),
-                dma((3,)),
                 dma((4,)),
                 dma(()),
                 dma(()),
-                dma((7,)),
-                dma((3,)),
-                dma((4,)),
                 dma(()),
+                dma((8,)),
+                dma((2,)),
+                dma((2,)),
                 dma(()),
+                dma((8,)),
+                dma((2,)),
+                dma((2,)),
                 dma((steps,)),
                 dma(()),
                 dma((nb,)),
@@ -820,6 +908,13 @@
             cotangent,
         )
     )
+    return tuple(
+        pl.pallas_call(
+            write_kernel,
+            out_shape=tuple(jax.ShapeDtypeStruct(o.shape, o.dtype) for o in outs),
+            name="write",
+        )(*outs)
+    )
 
 
 def solution(mesh):

time: 164 us -> 160 us (0.976)
  local copies, waits for them, and re-layouts: 7.1 us -> 1.38 us
  Pallas kernels: 156 us -> 158 us
    unnamed x4 -> x0, local copies, waits for them, and re-layouts: 5.72 us -> none
    pallas_call x0 -> x1, Pallas kernels: none -> 1.68 us  [body(): pl.pallas_call(write_kernel, out_shape=tuple((jax.ShapeDtypeStruct(o.shap...]
where the time goes in v4:
time: 160 us
  Pallas kernels  158 us (99%)
    pallas_call x1, Pallas kernels, body(): pl.pallas_call(layer_kernel, out_shape=(jax.ShapeDtypeStruct((rows_blk, w...  156 us

profile of v4, /device:TPU:1, one launch (start us, length us, event | category | flops | bytes accessed | tf_op | source)
XLA Modules:
  0.0 159.6 jit_solution(5091390631830016554)
XLA Ops:
  0.6 1.4 copy.16.coords_ref
  2.0 155.9 %layer.1 = (bf16[512,128]{1,0:T(8,128)(2,1)}, bf16[64,1024]{1,0:T(8,128)(2,1)}, f32[32,128]{1,0:T(8,128)}, f32[3,128]{1,0:T(4,128)}) custom-call(bf16[512,1024]{1,0:T(8,128)(2,1)} %feat_hbm.1, s32[1,512]{1,0:T(1,128)} %bitcast.9, bf16[4,4,256,256]{3,2,1,0:T(8,128)(2,1)} %bitcast.7, s32[4]{0:T(128)} %bitcast.10, s32[4,4,2]{2,1,0:T(4,128)} %copy.16.coords_ref, ...), custom_call_target="tpu_custom_call" | custom-call | tf_op jit(solution)/shard_map/layer/pallas_call | solution.py:808
  157.9 1.7 %write.1 = (bf16[512,128]{1,0:T(8,128)(2,1)}, bf16[64,1024]{1,0:T(8,128)(2,1)}, f32[32,128]{1,0:T(8,128)}, f32[3,128]{1,0:T(4,128)}) custom-call(bf16[512,128]{1,0:T(8,128)(2,1)} %get-tuple-element.8.refs_0_, bf16[64,1024]{1,0:T(8,128)(2,1)} %get-tuple-element.9.refs_1_, f32[32,128]{1,0:T(8,128)} %get-tuple-element.10.refs_2_, ...), custom_call_target="tpu_custom_call" | custom-call | tf_op jit(solution)/shard_map/write/pallas_call | solution.py:912

commit v5 on v4

--- a/solution.py
+++ b/solution.py
@@ -58,7 +58,7 @@
 
 
 ROW_TILE = 128
-COL_TILE = 256
+COL_TILE = 512
 BY_FIRST = (((0,), (0,)), ((), ()))
 BY_LAST = (((1,), (1,)), ((), ()))
 

time: 160 us -> 157 us (0.981)
  Pallas kernels: 158 us -> 155 us
    pallas_call x1, Pallas kernels: 156 us -> 154 us  [body(): pl.pallas_call(layer_kernel, out_shape=(jax.ShapeDtypeStruct((rows_blk, w...]
where the time goes in v5:
time: 157 us
  Pallas kernels  155 us (99%)
    pallas_call x1, Pallas kernels, body(): pl.pallas_call(layer_kernel, out_shape=(jax.ShapeDtypeStruct((rows_blk, w...  154 us

profile of v5, /device:TPU:1, one launch (start us, length us, event | category | flops | bytes accessed | tf_op | source)
XLA Modules:
  0.0 157.3 jit_solution(3031369295201401624)
XLA Ops:
  0.6 1.4 copy.16.coords_ref
  2.0 153.6 %layer.1 = (bf16[512,128]{1,0:T(8,128)(2,1)}, bf16[64,1024]{1,0:T(8,128)(2,1)}, f32[32,128]{1,0:T(8,128)}, f32[3,128]{1,0:T(4,128)}) custom-call(bf16[512,1024]{1,0:T(8,128)(2,1)} %feat_hbm.1, s32[1,512]{1,0:T(1,128)} %bitcast.9, bf16[4,4,256,256]{3,2,1,0:T(8,128)(2,1)} %bitcast.7, s32[4]{0:T(128)} %bitcast.10, s32[4,4,2]{2,1,0:T(4,128)} %copy.16.coords_ref, ...), custom_call_target="tpu_custom_call" | custom-call | tf_op jit(solution)/shard_map/layer/pallas_call | solution.py:808
  155.6 1.7 %write.1 = (bf16[512,128]{1,0:T(8,128)(2,1)}, bf16[64,1024]{1,0:T(8,128)(2,1)}, f32[32,128]{1,0:T(8,128)}, f32[3,128]{1,0:T(4,128)}) custom-call(bf16[512,128]{1,0:T(8,128)(2,1)} %get-tuple-element.8.refs_0_, bf16[64,1024]{1,0:T(8,128)(2,1)} %get-tuple-element.9.refs_1_, f32[32,128]{1,0:T(8,128)} %get-tuple-element.10.refs_2_, ...), custom_call_target="tpu_custom_call" | custom-call | tf_op jit(solution)/shard_map/write/pallas_call | solution.py:912
